TPU v7x, 128 devices: a whole 4x4x4 slice. The times are simulated.
128 devices in a mesh: shard: 8 (over y_lo, z), ctx: 8 (over y_hi, x), tp: 2 (over core).
Axes of the slice: x: 4, y: 4 (y_hi: 2, y_lo: 2; y = y_hi * 2 + y_lo), z: 4, core: 2. Of those that a mesh axis runs over, the one named last changes fastest.
Arguments:
- tokens: bfloat16 [8, 2048, 2048], P('shard', 'ctx'), may hold values from -6 to 6
- cotangent: bfloat16 [8, 2048, 2048], P('shard', 'ctx'), may hold values from -6 to 6
- seq_ids: int32 [8, 2048], P('shard'), may hold values from 0 to 1, as said below
- block_ids: int32 [8, 2048], P('shard'), may hold values from 0 to 7, as said below
- keep_layer: int32 [8], P('shard'), may hold values from 0 to 1, as said below
- gain_attn: float32 [2048], replicated, may hold values from 0.25 to 1.75
- gain_ffn: float32 [2048], replicated, may hold values from 0.25 to 1.75
- w_query: float32 [2048, 2048], P('shard', 'tp'), may hold values from -0.125 to 0.125
- w_key: float32 [2048, 512], P('shard', 'tp'), may hold values from -0.125 to 0.125
- w_value: float32 [2048, 512], P('shard', 'tp'), may hold values from -0.125 to 0.125
- w_out: float32 [2048, 2048], P('shard', 'tp'), may hold values from -0.75 to 0.75
- w_gate: float32 [2048, 5632], P('shard', 'tp'), may hold values from -0.125 to 0.125
- w_up: float32 [2048, 5632], P('shard', 'tp'), may hold values from -0.125 to 0.125
- w_down: float32 [2048, 5632], P('shard', 'tp'), may hold values from -0.078125 to 0.078125
Outputs:
- output: bfloat16 [8, 2048, 2048], P('shard', 'ctx')
- input_grad: bfloat16 [8, 2048, 2048], P('shard', 'ctx')
- grad_gain_attn: float32 [2048], P('shard')
- grad_gain_ffn: float32 [2048], P('shard')
- grad_query: float32 [2048, 2048], P('shard', 'tp')
- grad_key: float32 [2048, 512], P('shard', 'tp')
- grad_value: float32 [2048, 512], P('shard', 'tp')
- grad_out: float32 [2048, 2048], P('shard', 'tp')
- grad_gate: float32 [2048, 5632], P('shard', 'tp')
- grad_up: float32 [2048, 5632], P('shard', 'tp')
- grad_down: float32 [2048, 5632], P('shard', 'tp')
Inputs may be any that keep to these rules, and one draw needn't show every extreme that they name: `seq_ids`: each sample holds exactly two documents: id 0 on a leading run of fewer than min(256, 256) positions, id 1 on the rest. Blocks of 256 positions are counted from each document's start: block_ids[p] = (p - start of p's document) // 256. `keep_layer`: at least one sample runs the layer and at least one skips it.
All inputs are finite; a program needn't handle non-finite values.
Results may differ from a plain program's by a relative error of at most 0.02.
Values may be sent and summed in bfloat16 or wider, within the bound.
No kernel may reach another device: no remote copies, remote signals or barrier semaphores. Data moves between devices by JAX's collectives and lax.ppermute only.
A program may use at most 256 MiB of HBM per device.

v0:
```python
import jax
import jax.numpy as jnp
from jax import lax
from jax.sharding import Mesh, PartitionSpec as P

HD = 128
EPS = 1e-05
NEG = -1e30
F32 = jnp.float32
BF16 = jnp.bfloat16
SHARD = ("yl", "z")
SWAP = ((0, 1), (1, 0))


def half(value):
    return value.astype(BF16)


def mm(left, right):
    return jnp.dot(left, right, preferred_element_type=F32)


def mm_nt(left, right):
    return lax.dot_general(left, right, (((1,), (1,)), ((), ())), preferred_element_type=F32)


def mm_tn(left, right):
    return lax.dot_general(left, right, (((0,), (0,)), ((), ())), preferred_element_type=F32)


def swap_cores(value):
    return lax.ppermute(value, "tp", SWAP)


def shift_x(value, hop):
    return lax.ppermute(value, "x", [(i, (i + hop) % 4) for i in range(4)])


def gather_x(value):
    return [value] + [shift_x(value, -hop) for hop in (1, 2, 3)]


def scatter_x(chunks):
    moved = [shift_x(half(chunks[hop]), hop) for hop in (2, 1, 3)]
    return chunks[0] + moved[0].astype(F32) + moved[1].astype(F32) + moved[2].astype(F32)


def absolute(chunks, x_at):
    stacked = jnp.stack(chunks + chunks[:3])
    return lax.dynamic_slice_in_dim(stacked, (4 - x_at) % 4, 4, axis=0)


def rotate(value, cosine, sine):
    turned = jnp.concatenate([-value[..., HD // 2 :], value[..., : HD // 2]], axis=-1)
    return value * cosine + turned * sine


def unrotate(grad, cosine, sine):
    scaled = grad * sine
    return grad * cosine + jnp.concatenate(
        [scaled[..., HD // 2 :], -scaled[..., : HD // 2]], axis=-1
    )


def norm_root(value):
    return lax.rsqrt(jnp.mean(value * value, axis=-1, keepdims=True) + EPS)


def norm_backward(value, root, gain, grad):
    scaled = gain * grad
    grad_value = root * scaled - value * root**3 * jnp.mean(scaled * value, axis=-1, keepdims=True)
    return (grad_value, jnp.sum(grad * value * root, axis=0))


def per_device(
    tokens,
    cotangent,
    seq_ids,
    block_ids,
    keep_layer,
    gain_attn,
    gain_ffn,
    w_query,
    w_key,
    w_value,
    w_out,
    w_gate,
    w_up,
    w_down,
):
    core, x_at, y_at = (lax.axis_index("tp"), lax.axis_index("x"), lax.axis_index("yh"))
    first = core == 0
    rows = tokens.shape[1] // 2
    width = tokens.shape[2]
    keep = keep_layer[0].astype(F32)
    scale = HD ** (-0.5)
    side = x_at // 2
    at = x_at % 2
    wq = half(lax.dynamic_slice_in_dim(w_query, at * 512, 512, axis=1))
    wk = half(lax.dynamic_slice_in_dim(w_key, at * HD, HD, axis=1))
    wv = half(lax.dynamic_slice_in_dim(w_value, at * HD, HD, axis=1))
    wo = half(lax.dynamic_slice_in_dim(w_out, at * 512, 512, axis=1))
    pack0 = jnp.concatenate([wq[:, :256], wk, wo[:, :256]], axis=1)
    pack1 = jnp.concatenate([wq[:, 256:], wv, wo[:, 256:]], axis=1)
    lent = lax.ppermute(
        jnp.where(first, pack1, pack0),
        ("x", "tp"),
        [(2 * i + i // 2, 2 * i + 1 - i // 2) for i in range(4)],
    )
    pack = jnp.where(core == side, jnp.where(first, pack0, pack1), lent)
    pack = lax.all_gather(pack, SHARD, axis=0, tiled=True)
    pack_other = swap_cores(pack)
    att0 = jnp.where(first, pack, pack_other)
    att1 = jnp.where(first, pack_other, pack)
    full_qkv = jnp.concatenate([att0[:, :384], att1[:, :384]], axis=1)
    full_out = jnp.concatenate([att0[:, 384:], att1[:, 384:]], axis=1)
    units = w_gate.shape[1] // 4

    def hidden_units(weight):
        own = half(lax.dynamic_slice_in_dim(weight, x_at * units, units, axis=1))
        own = lax.all_gather(own, SHARD, axis=0, tiled=True)
        return (own, swap_cores(own))

    xval = lax.dynamic_slice_in_dim(tokens[0], core * rows, rows, axis=0).astype(F32)
    grad_top = lax.dynamic_slice_in_dim(cotangent[0], core * rows, rows, axis=0).astype(F32)
    root_attn = norm_root(xval)
    normed_attn = jnp.concatenate(gather_x(half(xval * root_attn * gain_attn)), axis=0)
    count = normed_attn.shape[0]

    def of_positions(line, y_index, core_index):
        grid = line.reshape(2, 4, 2, rows)
        picked = lax.dynamic_index_in_dim(grid, y_index, 0, keepdims=False)
        picked = lax.dynamic_index_in_dim(picked, core_index, 1, keepdims=False)
        double = jnp.concatenate([picked, picked], axis=0)
        return lax.dynamic_slice_in_dim(double, x_at, 4, axis=0).reshape(-1)

    corners = ((y_at, core), (y_at, 1 - core), (1 - y_at, core), (1 - y_at, 1 - core))
    seg_query = of_positions(seq_ids[0], y_at, core)
    blk_query = of_positions(block_ids[0], y_at, core)
    seg_keys = jnp.concatenate([of_positions(seq_ids[0], *corner) for corner in corners])
    blk_keys = jnp.concatenate([of_positions(block_ids[0], *corner) for corner in corners])
    allowed = (seg_query[:, None] == seg_keys[None, :]) & (blk_keys[None, :] <= blk_query[:, None])
    position = of_positions(jnp.arange(seq_ids.shape[1], dtype=jnp.int32), y_at, core)
    freqs = 10000.0 ** (-(jnp.arange(HD // 2).astype(F32) * 2.0 / HD))
    angle = position.astype(F32)[:, None] * freqs[None, :]
    cosine = jnp.concatenate([jnp.cos(angle), jnp.cos(angle)], axis=-1)
    sine = jnp.concatenate([jnp.sin(angle), jnp.sin(angle)], axis=-1)
    qkv = mm(normed_attn, full_qkv)
    starts = (0, 128, 384, 512)
    query = jnp.stack([half(rotate(qkv[:, s : s + HD], cosine, sine)) for s in starts])
    keys_values = jnp.concatenate(
        [half(rotate(qkv[:, 256:384], cosine, sine)), half(qkv[:, 640:])], axis=1
    )

    def across_y(value):
        return lax.ppermute(value, "yh", SWAP)

    two_kv = jnp.concatenate([keys_values, across_y(keys_values)], axis=0)
    other_kv = swap_cores(two_kv)
    all_kv = jnp.concatenate(
        [two_kv[:count], other_kv[:count], two_kv[count:], other_kv[count:]], axis=0
    )
    all_keys, all_values = (all_kv[:, :HD], all_kv[:, HD:])
    raw = jnp.einsum("htd,nd->htn", query, all_keys, preferred_element_type=F32) * scale
    safe = jnp.where(allowed[None], raw, NEG)
    top = jnp.max(safe, axis=-1, keepdims=True)
    weights = jnp.where(allowed[None], jnp.exp(safe - top), 0.0)
    total = jnp.sum(weights, axis=-1, keepdims=True)
    added = jnp.einsum("htn,nd->htd", half(weights), all_values, preferred_element_type=F32)
    heads_f = added / total
    log_total = top + jnp.log(total)
    heads = half(heads_f.transpose(1, 0, 2).reshape(count, 4 * HD))

    def chunked(value):
        return [value[j * rows : (j + 1) * rows] for j in range(4)]

    attn_branch = scatter_x(chunked(mm_nt(heads, full_out)))
    middle = xval + keep * attn_branch
    root_ffn = norm_root(middle)
    normed_ffn = jnp.concatenate(gather_x(half(middle * root_ffn * gain_ffn)), axis=0)
    full_gate, full_up, full_down = (hidden_units(w_gate), hidden_units(w_up), hidden_units(w_down))
    d_ffn = jnp.concatenate(gather_x(half(keep * grad_top)), axis=0)
    branch = 0.0
    d_normed = 0.0
    grads_gate, grads_up, grads_down = ([], [], [])
    for wg, wu, wd in zip(full_gate, full_up, full_down, strict=True):
        gate = mm(normed_ffn, wg)
        up = mm(normed_ffn, wu)
        sig = jax.nn.sigmoid(gate)
        silu = gate * sig
        hidden = half(silu * up)
        branch = branch + mm_nt(hidden, wd)
        d_hidden = mm(d_ffn, wd)
        d_gate = half(d_hidden * up * sig * (1.0 + gate * (1.0 - sig)))
        d_up = half(d_hidden * silu)
        d_normed = d_normed + mm_nt(d_gate, wg) + mm_nt(d_up, wu)
        grads_gate.append(mm_tn(normed_ffn, d_gate))
        grads_up.append(mm_tn(normed_ffn, d_up))
        grads_down.append(mm_tn(d_ffn, hidden))
    d_normed_ffn = scatter_x(chunked(d_normed))
    ffn_branch = scatter_x(chunked(branch))

    def both_cores(value):
        other = swap_cores(value)
        return jnp.concatenate(
            [jnp.where(first, value, other), jnp.where(first, other, value)], axis=0
        )

    output = both_cores(half(middle + keep * ffn_branch))

    def reduce_columns(mine, theirs):
        value = half(mine + swap_cores(half(theirs)).astype(F32))
        value = lax.psum_scatter(value, SHARD, scatter_dimension=0, tiled=True)
        value = half(value.astype(F32) + across_y(value).astype(F32))
        return absolute(gather_x(value), x_at)

    def units_of(value):
        return jnp.concatenate([value[i] for i in range(4)], axis=1).astype(F32)

    grad_down = units_of(reduce_columns(*grads_down))
    grad_gate = units_of(reduce_columns(*grads_gate))
    grad_up = units_of(reduce_columns(*grads_up))
    mid_part, gain_ffn_local = norm_backward(middle, root_ffn, gain_ffn, d_normed_ffn)
    d_middle = grad_top + mid_part
    d_attn = jnp.concatenate(gather_x(half(keep * d_middle)), axis=0)
    d_heads = half(mm(d_attn, full_out))
    d_heads_g = d_heads.reshape(count, 4, HD).transpose(1, 0, 2)
    row_delta = jnp.sum(d_heads_g.astype(F32) * heads_f, axis=-1, keepdims=True)
    raw = jnp.einsum("htd,nd->htn", query, all_keys, preferred_element_type=F32) * scale
    probs = jnp.where(allowed[None], jnp.exp(raw - log_total), 0.0)
    d_probs = jnp.einsum("htd,nd->htn", d_heads_g, all_values, preferred_element_type=F32)
    d_scores = half(scale * probs * (d_probs - row_delta))
    grad_q = jnp.einsum("htn,nd->htd", d_scores, all_keys, preferred_element_type=F32)
    key_part = jnp.einsum("htn,htd->nd", d_scores, query, preferred_element_type=F32)
    value_part = jnp.einsum("htn,htd->nd", half(probs), d_heads_g, preferred_element_type=F32)
    kv_part = jnp.concatenate([key_part, value_part], axis=1)
    kv_mine = jnp.concatenate([kv_part[:count], kv_part[2 * count : 3 * count]], axis=0)
    kv_theirs = jnp.concatenate([kv_part[count : 2 * count], kv_part[3 * count :]], axis=0)
    kv_two = kv_mine + swap_cores(half(kv_theirs)).astype(F32)
    grad_kv = kv_two[:count] + across_y(half(kv_two[count:])).astype(F32)
    d_q = [half(unrotate(grad_q[h], cosine, sine)) for h in range(4)]
    d_key = half(unrotate(grad_kv[:, :HD], cosine, sine))
    d_qkv = jnp.concatenate([d_q[0], d_q[1], d_key, d_q[2], d_q[3], half(grad_kv[:, HD:])], axis=1)
    d_normed_attn = scatter_x(chunked(mm_nt(d_qkv, full_qkv)))
    grad_qkv = mm_tn(normed_attn, d_qkv)
    grad_o = mm_tn(d_attn, heads)
    grads0 = jnp.concatenate([grad_qkv[:, :384], grad_o[:, :256]], axis=1)
    grads1 = jnp.concatenate([grad_qkv[:, 384:], grad_o[:, 256:]], axis=1)
    packs = reduce_columns(jnp.where(first, grads0, grads1), jnp.where(first, grads1, grads0))
    mine = lax.dynamic_slice_in_dim(packs, 2 * core, 2, axis=0)
    theirs = swap_cores(lax.dynamic_slice_in_dim(packs, 2 - 2 * core, 2, axis=0))
    out0 = jnp.where(first, mine, theirs).astype(F32)
    out1 = jnp.where(first, theirs, mine).astype(F32)
    grad_query = jnp.concatenate(
        [out0[0, :, :256], out1[0, :, :256], out0[1, :, :256], out1[1, :, :256]], axis=1
    )
    grad_key = jnp.concatenate([out0[0, :, 256:384], out0[1, :, 256:384]], axis=1)
    grad_value = jnp.concatenate([out1[0, :, 256:384], out1[1, :, 256:384]], axis=1)
    grad_out = jnp.concatenate(
        [out0[0, :, 384:], out1[0, :, 384:], out0[1, :, 384:], out1[1, :, 384:]], axis=1
    )
    input_part, gain_attn_local = norm_backward(xval, root_attn, gain_attn, d_normed_attn)
    input_grad = both_cores(half(d_middle + input_part))
    gains = lax.psum(jnp.stack([gain_attn_local, gain_ffn_local]), ("yl", "z", "yh", "x", "tp"))
    owned = width // 8
    gains = lax.dynamic_slice_in_dim(
        gains, (lax.axis_index("yl") * 4 + lax.axis_index("z")) * owned, owned, axis=1
    )
    return (
        output[None],
        input_grad[None],
        gains[0],
        gains[1],
        grad_query,
        grad_key,
        grad_value,
        grad_out,
        grad_gate,
        grad_up,
        grad_down,
    )


def solution(mesh):
    fine = Mesh(mesh.devices.reshape(2, 4, 2, 4, 2), ("yl", "z", "yh", "x", "tp"))
    shard, ctx = (("yl", "z"), ("yh", "x"))
    acts, weight = (P(shard, ctx, None), P(shard, "tp"))
    return jax.shard_map(
        per_device,
        mesh=fine,
        in_specs=(acts, acts, P(shard, None), P(shard, None), P(shard), P(), P()) + (weight,) * 7,
        out_specs=(acts, acts, P(shard), P(shard)) + (weight,) * 7,
        check_vma=False,
    )
```

profile of v0, /device:TPU:17, one launch (start us, length us, event | category | flops | bytes accessed | tf_op | source)
XLA Modules:
  0.0 724.8 jit_solution(15446372410941713195)
XLA Ops:
  25.9 42.6 %all-gather.5.cloned.1.call-done = bf16[2048,640]{0,1:T(8,128)(2,1)} async-done(((bf16[256,640]{0,1:T(8,128)(2,1)}), bf16[2048,640]{0,1:T(8,128)(2,1)}) %all-gather.5.cloned.1.call-update) | async-done | bytes 2621456 | tf_op jit(solution)/shard_map/all_gather | solution.py:111
  68.4 4.7 collective-permute-start.4
  89.1 12.2 %collective-permute-done.1 = bf16[128,2048]{1,0:T(8,128)(2,1)} collective-permute-done((bf16[128,2048]{1,0:T(8,128)(2,1)}, bf16[128,2048]{1,0:T(8,128)(2,1)}, u32[]{:S(2)}, u32[]{:S(2)}) %collective-permute-start.1) | collective-permute-done | bytes 524320 | tf_op jit(solution)/shard_map/ppermute | solution.py:36
  101.3 3.4 fusion.14
  108.0 12.4 %collective-permute-done.5 = bf16[512,256]{1,0:T(8,128)(2,1)S(1)} collective-permute-done((bf16[512,256]{1,0:T(8,128)(2,1)S(1)}, bf16[512,256]{1,0:T(8,128)(2,1)S(1)}, u32[]{:S(2)}, u32[]{:S(2)}) %collective-permute-start.5) | collective-permute-done | bytes 262176 | tf_op jit(solution)/shard_map/ppermute | solution.py:156
  124.2 2.7 all-gather.11.cloned.1.call-done
  126.9 5.1 collective-permute-start.15
  132.0 48.6 %all-gather.9.cloned.1.call-done = bf16[2048,704]{0,1:T(8,128)(2,1)} async-done(((bf16[256,704]{0,1:T(8,128)(2,1)}), bf16[2048,704]{0,1:T(8,128)(2,1)}) %all-gather.9.cloned.1.call-update) | async-done | bytes 2883600 | tf_op jit(solution)/shard_map/all_gather | solution.py:121
  180.6 4.9 collective-permute-start.14
  192.9 3.6 select_reduce_fusion
  196.5 5.0 fusion.1
  202.3 5.7 fusion.43
  208.0 3.3 fusion.129
  214.9 19.1 %all-gather.7.cloned.1.call-done = bf16[2048,704]{0,1:T(8,128)(2,1)} async-done(((bf16[256,704]{0,1:T(8,128)(2,1)}), bf16[2048,704]{0,1:T(8,128)(2,1)}) %all-gather.7.cloned.1.call-update) | async-done | bytes 2883600 | tf_op jit(solution)/shard_map/all_gather | solution.py:121
  234.0 5.0 collective-permute-start.13
  239.0 2.7 collective-permute-start.7
  243.6 10.8 %collective-permute-done.7 = bf16[128,2048]{1,0:T(8,128)(2,1)} collective-permute-done((bf16[128,2048]{1,0:T(8,128)(2,1)}, bf16[128,2048]{1,0:T(8,128)(2,1)}, u32[]{:S(2)}, u32[]{:S(2)}) %collective-permute-start.7) | collective-permute-done | bytes 524320 | tf_op jit(solution)/shard_map/ppermute | solution.py:36
  254.4 2.7 collective-permute-start.21
  259.2 6.9 collective-permute-done.22
  266.8 10.0 %collective-permute-done.21 = bf16[128,2048]{1,0:T(8,128)(2,1)S(1)} collective-permute-done((bf16[128,2048]{1,0:T(8,128)(2,1)}, bf16[128,2048]{1,0:T(8,128)(2,1)S(1)}, u32[]{:S(2)}, u32[]{:S(2)}) %collective-permute-start.21) | collective-permute-done | bytes 524320 | tf_op jit(solution)/shard_map/ppermute | solution.py:36
  276.8 4.0 collective-permute-done.20
  284.3 3.8 fusion.104
  290.6 11.6 %collective-permute-done.11 = bf16[128,2048]{1,0:T(8,128)(2,1)S(1)} collective-permute-done((bf16[128,2048]{1,0:T(8,128)(2,1)S(1)}, bf16[128,2048]{1,0:T(8,128)(2,1)S(1)}, u32[]{:S(2)}, u32[]{:S(2)}) %collective-permute-start.11) | collective-permute-done | bytes 524320 | tf_op jit(solution)/shard_map/ppermute | solution.py:36
  302.2 4.7 collective-permute-done.10
  307.0 3.7 fusion.106
  310.7 4.2 multiply_convert_fusion.2
  314.9 3.2 convolution_convert_fusion.2
  319.6 3.7 fusion.135
  326.9 3.5 multiply_convert_fusion.3
  334.1 4.1 fusion.112
  338.4 2.8 collective-permute-start.25
  344.4 5.8 fusion.130
  352.8 11.0 %collective-permute-done.25 = bf16[128,2048]{1,0:T(8,128)(2,1)S(1)} collective-permute-done((bf16[128,2048]{1,0:T(8,128)(2,1)S(1)}, bf16[128,2048]{1,0:T(8,128)(2,1)S(1)}, u32[]{:S(2)}, u32[]{:S(2)}) %collective-permute-start.25) | collective-permute-done | bytes 524320 | tf_op jit(solution)/shard_map/ppermute | solution.py:36
  363.8 3.2 collective-permute-done.24
  369.9 4.3 add_convert_fusion.2
  374.3 12.0 %collective-permute-done.18 = bf16[128,2048]{1,0:T(8,128)(2,1)S(1)} collective-permute-done((bf16[128,2048]{1,0:T(8,128)(2,1)}, bf16[128,2048]{1,0:T(8,128)(2,1)S(1)}, u32[]{:S(2)}, u32[]{:S(2)}) %collective-permute-start.18) | collective-permute-done | bytes 524320 | tf_op jit(solution)/shard_map/ppermute | solution.py:36
  386.4 4.6 collective-permute-done.16
  391.0 4.3 multiply_convert_fusion.7
  399.8 2.6 collective-permute-start.46
  402.4 4.5 convolution_convert_fusion
  408.5 14.0 %collective-permute-start.19 = (bf16[128,2048]{1,0:T(8,128)(2,1)}, bf16[128,2048]{1,0:T(8,128)(2,1)}, u32[]{:S(2)}, u32[]{:S(2)}) collective-permute-start(bf16[128,2048]{1,0:T(8,128)(2,1)} %get-tuple-element.127), channel_id=1, source_target_pairs={{0,1},{1,0},{2,3},{3,2},{4,5},{5,4},{6,7},{7,6},{8,9},{9,8},{10,11... | collective-permute-start | bytes 1572872 | tf_op jit(solution)/shard_map/ppermute | solution.py:32
  424.4 12.5 %multiply_convert_fusion = bf16[4,512,2048]{2,1,0:T(8,128)(2,1)} fusion(f32[4,512,2048]{2,1,0:T(8,128)} %copy-done.5, f32[4,512]{1,0:T(4,128)S(1)} %get-tuple-element.171, f32[4,512]{1,0:T(4,128)S(1)} %log_add_fusion, pred[512,2048]{1,0:T(8,128)(4,1)S(1)} %copy-done.13, bf16[4,512,128]{1,2,0:T(8,128)(2,1)S(1)} %bitcast.246, bf16[2048,256]{1,0:T(8,128)(2,1)S(1)} %copy-done.31), kind=kOutput, calls=%fused_computation | convolution fusion | flops 1103101952 | bytes 27279360 | tf_op jit(solution)/shard_map/htd,nd->htn/dot_general | solution.py:231
  436.9 5.8 convolution_bitcast_fusion
  442.8 8.1 %fusion.9 = f32[2048,128]{1,0:T(8,128)S(1)} fusion(bf16[4,512,128]{1,2,0:T(8,128)(2,1)S(1)} %bitcast.247, f32[4,512,2048]{2,1,0:T(8,128)} %copy-done.5, f32[4,512]{1,0:T(4,128)S(1)} %log_add_fusion, pred[512,2048]{1,0:T(8,128)(4,1)S(1)} %copy-done.13), kind=kOutput, calls=%fused_computation.33 | convolution fusion | flops 1090519040 | bytes 19406848 | tf_op jit(solution)/shard_map/htn,htd->nd/dot_general | solution.py:235
  452.9 3.0 add_convert_fusion.1
  465.5 10.9 %collective-permute-done.30 = bf16[512,256]{1,0:T(8,128)(2,1)S(1)} collective-permute-done((bf16[512,256]{1,0:T(8,128)(2,1)S(1)}, bf16[512,256]{1,0:T(8,128)(2,1)S(1)}, u32[]{:S(2)}, u32[]{:S(2)}) %collective-permute-start.30) | collective-permute-done | bytes 262176 | tf_op jit(solution)/shard_map/ppermute | solution.py:156
  479.4 5.5 add_convert_fusion
  486.6 3.2 fusion.131
  489.9 2.7 collective-permute-start.33
  494.1 3.4 fusion.48
  507.5 9.2 %collective-permute-done.31 = bf16[128,2048]{1,0:T(8,128)(2,1)S(1)} collective-permute-done((bf16[128,2048]{1,0:T(8,128)(2,1)S(1)}, bf16[128,2048]{1,0:T(8,128)(2,1)S(1)}, u32[]{:S(2)}, u32[]{:S(2)}) %collective-permute-start.31) | collective-permute-done | bytes 524320 | tf_op jit(solution)/shard_map/ppermute | solution.py:36
  518.7 2.8 collective-permute-start.34
  522.6 70.6 %psum.7 = f32[2,2048]{1,0:T(2,128)S(1)} all-reduce(f32[2,2048]{1,0:T(2,128)S(1)} %pad_maximum_fusion.34), channel_id=1, replica_groups=mesh['yl'=2,'z'=4,'yh'=2,'x'=4,'tp'=2] {'yl','z','yh','x','tp'}, use_global_device_ids=true, to_apply=%region_9.10 | all-reduce | flops 4096 | bytes 32768 | tf_op jit(solution)/shard_map/psum | solution.py:264
  596.6 5.7 add_convert_fusion.3
  602.4 2.6 collective-permute-start.47
  610.1 8.0 %collective-permute-done.47 = bf16[256,704]{0,1:T(8,128)(2,1)S(1)} collective-permute-done((bf16[256,704]{0,1:T(8,128)(2,1)}, bf16[256,704]{0,1:T(8,128)(2,1)S(1)}, u32[]{:S(2)}, u32[]{:S(2)}) %collective-permute-start.47) | collective-permute-done | bytes 360480 | tf_op jit(solution)/shard_map/ppermute | solution.py:156
  618.2 14.8 %collective-permute-done.52 = bf16[256,704]{0,1:T(8,128)(2,1)S(1)} collective-permute-done((bf16[256,704]{0,1:T(8,128)(2,1)}, bf16[256,704]{0,1:T(8,128)(2,1)S(1)}, u32[]{:S(2)}, u32[]{:S(2)}) %collective-permute-start.52) | collective-permute-done | bytes 360480 | tf_op jit(solution)/shard_map/ppermute | solution.py:156
  634.0 2.7 collective-permute-start.53
  640.9 14.2 %collective-permute-done.50 = bf16[256,704]{0,1:T(8,128)(2,1)S(1)} collective-permute-done((bf16[256,704]{0,1:T(8,128)(2,1)S(1)}, bf16[256,704]{0,1:T(8,128)(2,1)S(1)}, u32[]{:S(2)}, u32[]{:S(2)}) %collective-permute-start.50) | collective-permute-done | bytes 360480 | tf_op jit(solution)/shard_map/ppermute | solution.py:36
  659.8 7.6 %collective-permute-done.55 = bf16[256,704]{0,1:T(8,128)(2,1)} collective-permute-done((bf16[256,704]{0,1:T(8,128)(2,1)}, bf16[256,704]{0,1:T(8,128)(2,1)}, u32[]{:S(2)}, u32[]{:S(2)}) %collective-permute-start.55) | collective-permute-done | bytes 360480 | tf_op jit(solution)/shard_map/ppermute | solution.py:36
  674.2 3.5 collective-permute-done.37
  677.7 3.1 collective-permute-done.38
  680.9 9.2 %collective-permute-done.39 = bf16[256,640]{0,1:T(8,128)(2,1)S(1)} collective-permute-done((bf16[256,640]{0,1:T(8,128)(2,1)S(1)}, bf16[256,640]{0,1:T(8,128)(2,1)S(1)}, u32[]{:S(2)}, u32[]{:S(2)}) %collective-permute-start.39) | collective-permute-done | bytes 327712 | tf_op jit(solution)/shard_map/ppermute | solution.py:36
  696.0 3.4 copy.68
  (446 shorter events, 168.1 us)
Async XLA Ops:
  7.2 61.2 %all-gather.5.cloned.1.call-start = ((), (), s32[]{:S(2)}) async-start(), calls=%async_computation.4 | async-start | bytes 2949120 | tf_op jit(solution)/shard_map/all_gather | solution.py:111
  15.8 3.9 collective-permute-start.3
  21.5 105.4 %all-gather.11.cloned.1.call-start = ((), (), s32[]{:S(2)}) async-start(), calls=%async_computation.7 | async-start | bytes 3244032 | tf_op jit(solution)/shard_map/all_gather | solution.py:121
  22.7 157.9 %all-gather.9.cloned.1.call-start = ((), (), s32[]{:S(2)}) async-start(), calls=%async_computation.6 | async-start | bytes 3244032 | tf_op jit(solution)/shard_map/all_gather | solution.py:121
  25.1 208.9 %all-gather.7.cloned.1.call-start = ((), (), s32[]{:S(2)}) async-start(), calls=%async_computation.5 | async-start | bytes 3244032 | tf_op jit(solution)/shard_map/all_gather | solution.py:121
  68.4 14.1 %collective-permute-start.4 = (bf16[2048,640]{0,1:T(8,128)(2,1)}, bf16[2048,640]{0,1:T(8,128)(2,1)}, u32[]{:S(2)}, u32[]{:S(2)}) collective-permute-start(bf16[2048,640]{0,1:T(8,128)(2,1)} %all-gather.5.cloned.1.call-done), channel_id=1, source_target_pairs={{0,1},{1,0},{2,3},{3,2},{4,5},{5,4},{6,7},{7,6},{8,9},{9,8},{10,11... | collective-permute-start | bytes 7864328 | tf_op jit(solution)/shard_map/ppermute | solution.py:32
  74.1 15.1 %collective-permute-start.2 = (bf16[128,2048]{1,0:T(8,128)(2,1)}, bf16[128,2048]{1,0:T(8,128)(2,1)}, u32[]{:S(2)}, u32[]{:S(2)}) collective-permute-start(bf16[128,2048]{1,0:T(8,128)(2,1)} %fusion.23), channel_id=1, source_target_pairs={{0,2},{2,4},{4,6},{6,0},{1,3},{3,5},{5,7},{7,1},{8,10},{10,12},{12... | collective-permute-start | bytes 1572872 | tf_op jit(solution)/shard_map/ppermute | solution.py:36
  75.3 26.0 %collective-permute-start.1 = (bf16[128,2048]{1,0:T(8,128)(2,1)}, bf16[128,2048]{1,0:T(8,128)(2,1)}, u32[]{:S(2)}, u32[]{:S(2)}) collective-permute-start(bf16[128,2048]{1,0:T(8,128)(2,1)} %fusion.23), channel_id=1, source_target_pairs={{0,4},{2,6},{4,0},{6,2},{1,5},{3,7},{5,1},{7,3},{8,12},{10,14},{12... | collective-permute-start | bytes 1572872 | tf_op jit(solution)/shard_map/ppermute | solution.py:36
  77.7 23.6 %collective-permute-start = (bf16[128,2048]{1,0:T(8,128)(2,1)}, bf16[128,2048]{1,0:T(8,128)(2,1)}, u32[]{:S(2)}, u32[]{:S(2)}) collective-permute-start(bf16[128,2048]{1,0:T(8,128)(2,1)} %fusion.23), channel_id=1, source_target_pairs={{0,6},{2,0},{4,2},{6,4},{1,7},{3,1},{5,3},{7,5},{8,14},{10,8},{12,... | collective-permute-start | bytes 1572872 | tf_op jit(solution)/shard_map/ppermute | solution.py:36
  81.1 515.0 %reduce-scatter.7.cloned.1.call-start = ((), (), s32[]{:S(2)}) async-start(), calls=%async_computation.9 | async-start | bytes 3244032 | tf_op jit(solution)/shard_map/reduce_scatter | solution.py:213
  106.7 13.7 %collective-permute-start.5 = (bf16[512,256]{1,0:T(8,128)(2,1)S(1)}, bf16[512,256]{1,0:T(8,128)(2,1)S(1)}, u32[]{:S(2)}, u32[]{:S(2)}) collective-permute-start(bf16[512,256]{1,0:T(8,128)(2,1)S(1)} %pad_maximum_fusion.29), channel_id=1, source_target_pairs={{0,8},{8,0},{1,9},{9,1},{2,10},{10,2},{3,11},{11,3},{4,12},{12,4},... | collective-permute-start | bytes 786440 | tf_op jit(solution)/shard_map/ppermute | solution.py:156
  121.3 70.3 %collective-permute-start.6 = (bf16[1024,256]{1,0:T(8,128)(2,1)}, bf16[1024,256]{1,0:T(8,128)(2,1)}, u32[]{:S(2)}, u32[]{:S(2)}) collective-permute-start(bf16[1024,256]{1,0:T(8,128)(2,1)} %pad_maximum_fusion.19), channel_id=1, source_target_pairs={{0,1},{1,0},{2,3},{3,2},{4,5},{5,4},{6,7},{7,6},{8,9},{9,8},{10,11... | collective-permute-start | bytes 1572872 | tf_op jit(solution)/shard_map/ppermute | solution.py:32
  126.9 155.7 %collective-permute-start.15 = (bf16[2048,704]{0,1:T(8,128)(2,1)}, bf16[2048,704]{0,1:T(8,128)(2,1)}, u32[]{:S(2)}, u32[]{:S(2)}) collective-permute-start(bf16[2048,704]{0,1:T(8,128)(2,1)} %all-gather.11.cloned.1.call-done), channel_id=1, source_target_pairs={{0,1},{1,0},{2,3},{3,2},{4,5},{5,4},{6,7},{7,6},{8,9},{9,8},{10,11... | collective-permute-start | bytes 8650760 | tf_op jit(solution)/shard_map/ppermute | solution.py:32
  180.6 107.6 %collective-permute-start.14 = (bf16[2048,704]{0,1:T(8,128)(2,1)}, bf16[2048,704]{0,1:T(8,128)(2,1)}, u32[]{:S(2)}, u32[]{:S(2)}) collective-permute-start(bf16[2048,704]{0,1:T(8,128)(2,1)} %all-gather.9.cloned.1.call-done), channel_id=1, source_target_pairs={{0,1},{1,0},{2,3},{3,2},{4,5},{5,4},{6,7},{7,6},{8,9},{9,8},{10,11... | collective-permute-start | bytes 8650760 | tf_op jit(solution)/shard_map/ppermute | solution.py:32
  212.5 26.5 %collective-permute-start.9 = (bf16[128,2048]{1,0:T(8,128)(2,1)}, bf16[128,2048]{1,0:T(8,128)(2,1)S(1)}, u32[]{:S(2)}, u32[]{:S(2)}) collective-permute-start(bf16[128,2048]{1,0:T(8,128)(2,1)} %get-tuple-element.91), channel_id=1, source_target_pairs={{0,6},{2,0},{4,2},{6,4},{1,7},{3,1},{5,3},{7,5},{8,14},{10,8},{12,... | collective-permute-start | bytes 1572872 | tf_op jit(solution)/shard_map/ppermute | solution.py:36
  214.9 28.3 %collective-permute-start.8 = (bf16[128,2048]{1,0:T(8,128)(2,1)}, bf16[128,2048]{1,0:T(8,128)(2,1)}, u32[]{:S(2)}, u32[]{:S(2)}) collective-permute-start(bf16[128,2048]{1,0:T(8,128)(2,1)} %get-tuple-element.92), channel_id=1, source_target_pairs={{0,2},{2,4},{4,6},{6,0},{1,3},{3,5},{5,7},{7,1},{8,10},{10,12},{12... | collective-permute-start | bytes 1572872 | tf_op jit(solution)/shard_map/ppermute | solution.py:36
  234.0 76.7 %collective-permute-start.13 = (bf16[2048,704]{0,1:T(8,128)(2,1)}, bf16[2048,704]{0,1:T(8,128)(2,1)}, u32[]{:S(2)}, u32[]{:S(2)}) collective-permute-start(bf16[2048,704]{0,1:T(8,128)(2,1)} %all-gather.7.cloned.1.call-done), channel_id=1, source_target_pairs={{0,1},{1,0},{2,3},{3,2},{4,5},{5,4},{6,7},{7,6},{8,9},{9,8},{10,11... | collective-permute-start | bytes 8650760 | tf_op jit(solution)/shard_map/ppermute | solution.py:32
  239.0 15.4 %collective-permute-start.7 = (bf16[128,2048]{1,0:T(8,128)(2,1)}, bf16[128,2048]{1,0:T(8,128)(2,1)}, u32[]{:S(2)}, u32[]{:S(2)}) collective-permute-start(bf16[128,2048]{1,0:T(8,128)(2,1)} %get-tuple-element.90), channel_id=1, source_target_pairs={{0,4},{2,6},{4,0},{6,2},{1,5},{3,7},{5,1},{7,3},{8,12},{10,14},{12... | collective-permute-start | bytes 1572872 | tf_op jit(solution)/shard_map/ppermute | solution.py:36
  243.3 22.9 %collective-permute-start.22 = (bf16[128,2048]{1,0:T(8,128)(2,1)}, bf16[128,2048]{1,0:T(8,128)(2,1)}, u32[]{:S(2)}, u32[]{:S(2)}) collective-permute-start(bf16[128,2048]{1,0:T(8,128)(2,1)} %fusion.20), channel_id=1, source_target_pairs={{0,2},{2,4},{4,6},{6,0},{1,3},{3,5},{5,7},{7,1},{8,10},{10,12},{12... | collective-permute-start | bytes 1572872 | tf_op jit(solution)/shard_map/ppermute | solution.py:36
  254.4 22.4 %collective-permute-start.21 = (bf16[128,2048]{1,0:T(8,128)(2,1)}, bf16[128,2048]{1,0:T(8,128)(2,1)S(1)}, u32[]{:S(2)}, u32[]{:S(2)}) collective-permute-start(bf16[128,2048]{1,0:T(8,128)(2,1)} %fusion.20), channel_id=1, source_target_pairs={{0,4},{2,6},{4,0},{6,2},{1,5},{3,7},{5,1},{7,3},{8,12},{10,14},{12... | collective-permute-start | bytes 1572872 | tf_op jit(solution)/shard_map/ppermute | solution.py:36
  266.2 14.6 %collective-permute-start.20 = (bf16[128,2048]{1,0:T(8,128)(2,1)}, bf16[128,2048]{1,0:T(8,128)(2,1)S(1)}, u32[]{:S(2)}, u32[]{:S(2)}) collective-permute-start(bf16[128,2048]{1,0:T(8,128)(2,1)} %fusion.20), channel_id=1, source_target_pairs={{0,6},{2,0},{4,2},{6,4},{1,7},{3,1},{5,3},{7,5},{8,14},{10,8},{12,... | collective-permute-start | bytes 1572872 | tf_op jit(solution)/shard_map/ppermute | solution.py:36
  276.8 13.9 %collective-permute-start.12 = (bf16[128,2048]{1,0:T(8,128)(2,1)S(1)}, bf16[128,2048]{1,0:T(8,128)(2,1)S(1)}, u32[]{:S(2)}, u32[]{:S(2)}) collective-permute-start(bf16[128,2048]{1,0:T(8,128)(2,1)S(1)} %multiply_convert_fusion.8), channel_id=1, source_target_pairs={{0,2},{2,4},{4,6},{6,0},{1,3},{3,5},{5,7},{7,1},{8,10},{10,12},{12... | collective-permute-start | bytes 1572872 | tf_op jit(solution)/shard_map/ppermute | solution.py:36
  280.8 21.4 %collective-permute-start.11 = (bf16[128,2048]{1,0:T(8,128)(2,1)S(1)}, bf16[128,2048]{1,0:T(8,128)(2,1)S(1)}, u32[]{:S(2)}, u32[]{:S(2)}) collective-permute-start(bf16[128,2048]{1,0:T(8,128)(2,1)S(1)} %multiply_convert_fusion.8), channel_id=1, source_target_pairs={{0,4},{2,6},{4,0},{6,2},{1,5},{3,7},{5,1},{7,3},{8,12},{10,14},{12... | collective-permute-start | bytes 1572872 | tf_op jit(solution)/shard_map/ppermute | solution.py:36
  282.6 24.4 %collective-permute-start.10 = (bf16[128,2048]{1,0:T(8,128)(2,1)S(1)}, bf16[128,2048]{1,0:T(8,128)(2,1)S(1)}, u32[]{:S(2)}, u32[]{:S(2)}) collective-permute-start(bf16[128,2048]{1,0:T(8,128)(2,1)S(1)} %multiply_convert_fusion.8), channel_id=1, source_target_pairs={{0,6},{2,0},{4,2},{6,4},{1,7},{3,1},{5,3},{7,5},{8,14},{10,8},{12,... | collective-permute-start | bytes 1572872 | tf_op jit(solution)/shard_map/ppermute | solution.py:36
  318.1 51.7 %collective-permute-start.41 = (bf16[2048,704]{0,1:T(8,128)(2,1)}, bf16[2048,704]{0,1:T(8,128)(2,1)}, u32[]{:S(2)}, u32[]{:S(2)}) collective-permute-start(bf16[2048,704]{0,1:T(8,128)(2,1)} %convolution_convert_fusion.2), channel_id=1, source_target_pairs={{0,1},{1,0},{2,3},{3,2},{4,5},{5,4},{6,7},{7,6},{8,9},{9,8},{10,11... | collective-permute-start | bytes 8650760 | tf_op jit(solution)/shard_map/ppermute | solution.py:32
  338.4 25.3 %collective-permute-start.25 = (bf16[128,2048]{1,0:T(8,128)(2,1)S(1)}, bf16[128,2048]{1,0:T(8,128)(2,1)S(1)}, u32[]{:S(2)}, u32[]{:S(2)}) collective-permute-start(bf16[128,2048]{1,0:T(8,128)(2,1)S(1)} %get-tuple-element.85), channel_id=1, source_target_pairs={{0,6},{2,0},{4,2},{6,4},{1,7},{3,1},{5,3},{7,5},{8,14},{10,8},{12,... | collective-permute-start | bytes 1572872 | tf_op jit(solution)/shard_map/ppermute | solution.py:36
  341.3 25.7 %collective-permute-start.24 = (bf16[128,2048]{1,0:T(8,128)(2,1)S(1)}, bf16[128,2048]{1,0:T(8,128)(2,1)S(1)}, u32[]{:S(2)}, u32[]{:S(2)}) collective-permute-start(bf16[128,2048]{1,0:T(8,128)(2,1)S(1)} %get-tuple-element.86), channel_id=1, source_target_pairs={{0,2},{2,4},{4,6},{6,0},{1,3},{3,5},{5,7},{7,1},{8,10},{10,12},{12... | collective-permute-start | bytes 1572872 | tf_op jit(solution)/shard_map/ppermute | solution.py:36
  341.3 27.2 %collective-permute-start.23 = (bf16[128,2048]{1,0:T(8,128)(2,1)S(1)}, bf16[128,2048]{1,0:T(8,128)(2,1)S(1)}, u32[]{:S(2)}, u32[]{:S(2)}) collective-permute-start(bf16[128,2048]{1,0:T(8,128)(2,1)S(1)} %get-tuple-element.84), channel_id=1, source_target_pairs={{0,4},{2,6},{4,0},{6,2},{1,5},{3,7},{5,1},{7,3},{8,12},{10,14},{12... | collective-permute-start | bytes 1572872 | tf_op jit(solution)/shard_map/ppermute | solution.py:36
  351.4 35.0 %collective-permute-start.18 = (bf16[128,2048]{1,0:T(8,128)(2,1)}, bf16[128,2048]{1,0:T(8,128)(2,1)S(1)}, u32[]{:S(2)}, u32[]{:S(2)}) collective-permute-start(bf16[128,2048]{1,0:T(8,128)(2,1)} %get-tuple-element.88), channel_id=1, source_target_pairs={{0,6},{2,0},{4,2},{6,4},{1,7},{3,1},{5,3},{7,5},{8,14},{10,8},{12,... | collective-permute-start | bytes 1572872 | tf_op jit(solution)/shard_map/ppermute | solution.py:36
  363.8 22.6 %collective-permute-start.17 = (bf16[128,2048]{1,0:T(8,128)(2,1)}, bf16[128,2048]{1,0:T(8,128)(2,1)}, u32[]{:S(2)}, u32[]{:S(2)}) collective-permute-start(bf16[128,2048]{1,0:T(8,128)(2,1)} %get-tuple-element.89), channel_id=1, source_target_pairs={{0,2},{2,4},{4,6},{6,0},{1,3},{3,5},{5,7},{7,1},{8,10},{10,12},{12... | collective-permute-start | bytes 1572872 | tf_op jit(solution)/shard_map/ppermute | solution.py:36
  367.0 23.9 %collective-permute-start.16 = (bf16[128,2048]{1,0:T(8,128)(2,1)}, bf16[128,2048]{1,0:T(8,128)(2,1)}, u32[]{:S(2)}, u32[]{:S(2)}) collective-permute-start(bf16[128,2048]{1,0:T(8,128)(2,1)} %get-tuple-element.87), channel_id=1, source_target_pairs={{0,4},{2,6},{4,0},{6,2},{1,5},{3,7},{5,1},{7,3},{8,12},{10,14},{12... | collective-permute-start | bytes 1572872 | tf_op jit(solution)/shard_map/ppermute | solution.py:36
  374.2 228.1 %reduce-scatter.9.cloned.1.call-start = ((), (), s32[]{:S(2)}) async-start(), calls=%async_computation.10 | async-start | bytes 3244032 | tf_op jit(solution)/shard_map/reduce_scatter | solution.py:213
  395.3 13.3 %collective-permute-start.28 = (bf16[128,2048]{1,0:T(8,128)(2,1)S(1)}, bf16[128,2048]{1,0:T(8,128)(2,1)S(1)}, u32[]{:S(2)}, u32[]{:S(2)}) collective-permute-start(bf16[128,2048]{1,0:T(8,128)(2,1)S(1)} %get-tuple-element.46), channel_id=1, source_target_pairs={{0,2},{2,4},{4,6},{6,0},{1,3},{3,5},{5,7},{7,1},{8,10},{10,12},{12... | collective-permute-start | bytes 1572872 | tf_op jit(solution)/shard_map/ppermute | solution.py:36
  395.3 27.2 %collective-permute-start.27 = (bf16[128,2048]{1,0:T(8,128)(2,1)S(1)}, bf16[128,2048]{1,0:T(8,128)(2,1)S(1)}, u32[]{:S(2)}, u32[]{:S(2)}) collective-permute-start(bf16[128,2048]{1,0:T(8,128)(2,1)S(1)} %get-tuple-element.46), channel_id=1, source_target_pairs={{0,4},{2,6},{4,0},{6,2},{1,5},{3,7},{5,1},{7,3},{8,12},{10,14},{12... | collective-permute-start | bytes 1572872 | tf_op jit(solution)/shard_map/ppermute | solution.py:36
  396.1 26.4 %collective-permute-start.26 = (bf16[128,2048]{1,0:T(8,128)(2,1)S(1)}, bf16[128,2048]{1,0:T(8,128)(2,1)S(1)}, u32[]{:S(2)}, u32[]{:S(2)}) collective-permute-start(bf16[128,2048]{1,0:T(8,128)(2,1)S(1)} %get-tuple-element.46), channel_id=1, source_target_pairs={{0,6},{2,0},{4,2},{6,4},{1,7},{3,1},{5,3},{7,5},{8,14},{10,8},{12,... | collective-permute-start | bytes 1572872 | tf_op jit(solution)/shard_map/ppermute | solution.py:36
  399.8 52.3 %collective-permute-start.46 = (bf16[2048,704]{0,1:T(8,128)(2,1)S(1)}, bf16[2048,704]{0,1:T(8,128)(2,1)S(1)}, u32[]{:S(2)}, u32[]{:S(2)}) collective-permute-start(bf16[2048,704]{0,1:T(8,128)(2,1)S(1)} %convolution_convert_fusion.1), channel_id=1, source_target_pairs={{0,1},{1,0},{2,3},{3,2},{4,5},{5,4},{6,7},{7,6},{8,9},{9,8},{10,11... | collective-permute-start | bytes 8650760 | tf_op jit(solution)/shard_map/ppermute | solution.py:32
  406.9 72.5 %collective-permute-start.51 = (bf16[2048,704]{0,1:T(8,128)(2,1)}, bf16[2048,704]{0,1:T(8,128)(2,1)}, u32[]{:S(2)}, u32[]{:S(2)}) collective-permute-start(bf16[2048,704]{0,1:T(8,128)(2,1)} %convolution_convert_fusion), channel_id=1, source_target_pairs={{0,1},{1,0},{2,3},{3,2},{4,5},{5,4},{6,7},{7,6},{8,9},{9,8},{10,11... | collective-permute-start | bytes 8650760 | tf_op jit(solution)/shard_map/ppermute | solution.py:32
  408.5 95.5 %collective-permute-start.19 = (bf16[128,2048]{1,0:T(8,128)(2,1)}, bf16[128,2048]{1,0:T(8,128)(2,1)}, u32[]{:S(2)}, u32[]{:S(2)}) collective-permute-start(bf16[128,2048]{1,0:T(8,128)(2,1)} %get-tuple-element.127), channel_id=1, source_target_pairs={{0,1},{1,0},{2,3},{3,2},{4,5},{5,4},{6,7},{7,6},{8,9},{9,8},{10,11... | collective-permute-start | bytes 1572872 | tf_op jit(solution)/shard_map/ppermute | solution.py:32
  455.9 150.1 %reduce-scatter.11.cloned.1.call-start = ((), (), s32[]{:S(2)}) async-start(), calls=%async_computation.11 | async-start | bytes 3244032 | tf_op jit(solution)/shard_map/reduce_scatter | solution.py:213
  457.2 4.2 collective-permute-start.29
  461.6 14.7 %collective-permute-start.30 = (bf16[512,256]{1,0:T(8,128)(2,1)S(1)}, bf16[512,256]{1,0:T(8,128)(2,1)S(1)}, u32[]{:S(2)}, u32[]{:S(2)}) collective-permute-start(bf16[512,256]{1,0:T(8,128)(2,1)S(1)} %slice.636), channel_id=1, source_target_pairs={{0,8},{8,0},{1,9},{9,1},{2,10},{10,2},{3,11},{11,3},{4,12},{12,4},... | collective-permute-start | bytes 786440 | tf_op jit(solution)/shard_map/ppermute | solution.py:156
  484.9 174.0 %reduce-scatter.5.cloned.1.call-start = ((), (), s32[]{:S(2)}) async-start(), calls=%async_computation.8 | async-start | bytes 2949120 | tf_op jit(solution)/shard_map/reduce_scatter | solution.py:213
  489.9 15.3 %collective-permute-start.33 = (bf16[128,2048]{1,0:T(8,128)(2,1)S(1)}, bf16[128,2048]{1,0:T(8,128)(2,1)S(1)}, u32[]{:S(2)}, u32[]{:S(2)}) collective-permute-start(bf16[128,2048]{1,0:T(8,128)(2,1)S(1)} %get-tuple-element.80), channel_id=1, source_target_pairs={{0,6},{2,0},{4,2},{6,4},{1,7},{3,1},{5,3},{7,5},{8,14},{10,8},{12,... | collective-permute-start | bytes 1572872 | tf_op jit(solution)/shard_map/ppermute | solution.py:36
  492.6 14.8 %collective-permute-start.32 = (bf16[128,2048]{1,0:T(8,128)(2,1)S(1)}, bf16[128,2048]{1,0:T(8,128)(2,1)S(1)}, u32[]{:S(2)}, u32[]{:S(2)}) collective-permute-start(bf16[128,2048]{1,0:T(8,128)(2,1)S(1)} %get-tuple-element.81), channel_id=1, source_target_pairs={{0,2},{2,4},{4,6},{6,0},{1,3},{3,5},{5,7},{7,1},{8,10},{10,12},{12... | collective-permute-start | bytes 1572872 | tf_op jit(solution)/shard_map/ppermute | solution.py:36
  492.7 24.0 %collective-permute-start.31 = (bf16[128,2048]{1,0:T(8,128)(2,1)S(1)}, bf16[128,2048]{1,0:T(8,128)(2,1)S(1)}, u32[]{:S(2)}, u32[]{:S(2)}) collective-permute-start(bf16[128,2048]{1,0:T(8,128)(2,1)S(1)} %get-tuple-element.79), channel_id=1, source_target_pairs={{0,4},{2,6},{4,0},{6,2},{1,5},{3,7},{5,1},{7,3},{8,12},{10,14},{12... | collective-permute-start | bytes 1572872 | tf_op jit(solution)/shard_map/ppermute | solution.py:36
  502.9 93.7 %collective-permute-start.35 = (bf16[2048,640]{0,1:T(8,128)(2,1)}, bf16[2048,640]{0,1:T(8,128)(2,1)}, u32[]{:S(2)}, u32[]{:S(2)}) collective-permute-start(bf16[2048,640]{0,1:T(8,128)(2,1)} %select_convert_fusion), channel_id=1, source_target_pairs={{0,1},{1,0},{2,3},{3,2},{4,5},{5,4},{6,7},{7,6},{8,9},{9,8},{10,11... | collective-permute-start | bytes 7864328 | tf_op jit(solution)/shard_map/ppermute | solution.py:32
  518.7 75.1 %collective-permute-start.34 = (bf16[128,2048]{1,0:T(8,128)(2,1)}, bf16[128,2048]{1,0:T(8,128)(2,1)}, u32[]{:S(2)}, u32[]{:S(2)}) collective-permute-start(bf16[128,2048]{1,0:T(8,128)(2,1)} %fusion.27), channel_id=1, source_target_pairs={{0,1},{1,0},{2,3},{3,2},{4,5},{5,4},{6,7},{7,6},{8,9},{9,8},{10,11... | collective-permute-start | bytes 1572872 | tf_op jit(solution)/shard_map/ppermute | solution.py:32
  596.1 11.0 %collective-permute-start.42 = (bf16[256,704]{0,1:T(8,128)(2,1)}, bf16[256,704]{0,1:T(8,128)(2,1)S(1)}, u32[]{:S(2)}, u32[]{:S(2)}) collective-permute-start(bf16[256,704]{0,1:T(8,128)(2,1)} %reduce-scatter.7.cloned.1.call-done), channel_id=1, source_target_pairs={{0,8},{8,0},{1,9},{9,1},{2,10},{10,2},{3,11},{11,3},{4,12},{12,4},... | collective-permute-start | bytes 1081352 | tf_op jit(solution)/shard_map/ppermute | solution.py:156
  602.4 15.6 %collective-permute-start.47 = (bf16[256,704]{0,1:T(8,128)(2,1)}, bf16[256,704]{0,1:T(8,128)(2,1)S(1)}, u32[]{:S(2)}, u32[]{:S(2)}) collective-permute-start(bf16[256,704]{0,1:T(8,128)(2,1)} %reduce-scatter.9.cloned.1.call-done), channel_id=1, source_target_pairs={{0,8},{8,0},{1,9},{9,1},{2,10},{10,2},{3,11},{11,3},{4,12},{12,4},... | collective-permute-start | bytes 1081352 | tf_op jit(solution)/shard_map/ppermute | solution.py:156
  606.0 27.0 %collective-permute-start.52 = (bf16[256,704]{0,1:T(8,128)(2,1)}, bf16[256,704]{0,1:T(8,128)(2,1)S(1)}, u32[]{:S(2)}, u32[]{:S(2)}) collective-permute-start(bf16[256,704]{0,1:T(8,128)(2,1)} %reduce-scatter.11.cloned.1.call-done), channel_id=1, source_target_pairs={{0,8},{8,0},{1,9},{9,1},{2,10},{10,2},{3,11},{11,3},{4,12},{12,4},... | collective-permute-start | bytes 1081352 | tf_op jit(solution)/shard_map/ppermute | solution.py:156
  607.2 26.8 %collective-permute-start.43 = (bf16[256,704]{0,1:T(8,128)(2,1)S(1)}, bf16[256,704]{0,1:T(8,128)(2,1)S(1)}, u32[]{:S(2)}, u32[]{:S(2)}) collective-permute-start(bf16[256,704]{0,1:T(8,128)(2,1)S(1)} %get-tuple-element.42), channel_id=1, source_target_pairs={{0,6},{2,0},{4,2},{6,4},{1,7},{3,1},{5,3},{7,5},{8,14},{10,8},{12,... | collective-permute-start | bytes 1081352 | tf_op jit(solution)/shard_map/ppermute | solution.py:36
  608.0 26.1 %collective-permute-start.44 = (bf16[256,704]{0,1:T(8,128)(2,1)S(1)}, bf16[256,704]{0,1:T(8,128)(2,1)S(1)}, u32[]{:S(2)}, u32[]{:S(2)}) collective-permute-start(bf16[256,704]{0,1:T(8,128)(2,1)S(1)} %get-tuple-element.42), channel_id=1, source_target_pairs={{0,4},{2,6},{4,0},{6,2},{1,5},{3,7},{5,1},{7,3},{8,12},{10,14},{12... | collective-permute-start | bytes 1081352 | tf_op jit(solution)/shard_map/ppermute | solution.py:36
  609.3 27.5 %collective-permute-start.45 = (bf16[256,704]{0,1:T(8,128)(2,1)S(1)}, bf16[256,704]{0,1:T(8,128)(2,1)S(1)}, u32[]{:S(2)}, u32[]{:S(2)}) collective-permute-start(bf16[256,704]{0,1:T(8,128)(2,1)S(1)} %get-tuple-element.42), channel_id=1, source_target_pairs={{0,2},{2,4},{4,6},{6,0},{1,3},{3,5},{5,7},{7,1},{8,10},{10,12},{12... | collective-permute-start | bytes 1081352 | tf_op jit(solution)/shard_map/ppermute | solution.py:36
  618.1 20.7 %collective-permute-start.48 = (bf16[256,704]{0,1:T(8,128)(2,1)S(1)}, bf16[256,704]{0,1:T(8,128)(2,1)S(1)}, u32[]{:S(2)}, u32[]{:S(2)}) collective-permute-start(bf16[256,704]{0,1:T(8,128)(2,1)S(1)} %get-tuple-element.40), channel_id=1, source_target_pairs={{0,6},{2,0},{4,2},{6,4},{1,7},{3,1},{5,3},{7,5},{8,14},{10,8},{12,... | collective-permute-start | bytes 1081352 | tf_op jit(solution)/shard_map/ppermute | solution.py:36
  633.0 7.9 %collective-permute-start.49 = (bf16[256,704]{0,1:T(8,128)(2,1)S(1)}, bf16[256,704]{0,1:T(8,128)(2,1)S(1)}, u32[]{:S(2)}, u32[]{:S(2)}) collective-permute-start(bf16[256,704]{0,1:T(8,128)(2,1)S(1)} %get-tuple-element.40), channel_id=1, source_target_pairs={{0,4},{2,6},{4,0},{6,2},{1,5},{3,7},{5,1},{7,3},{8,12},{10,14},{12... | collective-permute-start | bytes 1081352 | tf_op jit(solution)/shard_map/ppermute | solution.py:36
  634.0 21.2 %collective-permute-start.50 = (bf16[256,704]{0,1:T(8,128)(2,1)S(1)}, bf16[256,704]{0,1:T(8,128)(2,1)S(1)}, u32[]{:S(2)}, u32[]{:S(2)}) collective-permute-start(bf16[256,704]{0,1:T(8,128)(2,1)S(1)} %get-tuple-element.40), channel_id=1, source_target_pairs={{0,2},{2,4},{4,6},{6,0},{1,3},{3,5},{5,7},{7,1},{8,10},{10,12},{12... | collective-permute-start | bytes 1081352 | tf_op jit(solution)/shard_map/ppermute | solution.py:36
  634.0 23.4 %collective-permute-start.53 = (bf16[256,704]{0,1:T(8,128)(2,1)}, bf16[256,704]{0,1:T(8,128)(2,1)S(1)}, u32[]{:S(2)}, u32[]{:S(2)}) collective-permute-start(bf16[256,704]{0,1:T(8,128)(2,1)} %get-tuple-element.38), channel_id=1, source_target_pairs={{0,6},{2,0},{4,2},{6,4},{1,7},{3,1},{5,3},{7,5},{8,14},{10,8},{12,... | collective-permute-start | bytes 1081352 | tf_op jit(solution)/shard_map/ppermute | solution.py:36
  636.8 22.2 %collective-permute-start.54 = (bf16[256,704]{0,1:T(8,128)(2,1)}, bf16[256,704]{0,1:T(8,128)(2,1)S(1)}, u32[]{:S(2)}, u32[]{:S(2)}) collective-permute-start(bf16[256,704]{0,1:T(8,128)(2,1)} %get-tuple-element.38), channel_id=1, source_target_pairs={{0,4},{2,6},{4,0},{6,2},{1,5},{3,7},{5,1},{7,3},{8,12},{10,14},{12... | collective-permute-start | bytes 1081352 | tf_op jit(solution)/shard_map/ppermute | solution.py:36
  638.8 28.6 %collective-permute-start.55 = (bf16[256,704]{0,1:T(8,128)(2,1)}, bf16[256,704]{0,1:T(8,128)(2,1)}, u32[]{:S(2)}, u32[]{:S(2)}) collective-permute-start(bf16[256,704]{0,1:T(8,128)(2,1)} %get-tuple-element.38), channel_id=1, source_target_pairs={{0,2},{2,4},{4,6},{6,0},{1,3},{3,5},{5,7},{7,1},{8,10},{10,12},{12... | collective-permute-start | bytes 1081352 | tf_op jit(solution)/shard_map/ppermute | solution.py:36
  659.0 10.1 %collective-permute-start.36 = (bf16[256,640]{0,1:T(8,128)(2,1)}, bf16[256,640]{0,1:T(8,128)(2,1)S(1)}, u32[]{:S(2)}, u32[]{:S(2)}) collective-permute-start(bf16[256,640]{0,1:T(8,128)(2,1)} %reduce-scatter.5.cloned.1.call-done), channel_id=1, source_target_pairs={{0,8},{8,0},{1,9},{9,1},{2,10},{10,2},{3,11},{11,3},{4,12},{12,4},... | collective-permute-start | bytes 983048 | tf_op jit(solution)/shard_map/ppermute | solution.py:156
  670.2 7.5 %collective-permute-start.37 = (bf16[256,640]{0,1:T(8,128)(2,1)S(1)}, bf16[256,640]{0,1:T(8,128)(2,1)S(1)}, u32[]{:S(2)}, u32[]{:S(2)}) collective-permute-start(bf16[256,640]{0,1:T(8,128)(2,1)S(1)} %get-tuple-element.44), channel_id=1, source_target_pairs={{0,6},{2,0},{4,2},{6,4},{1,7},{3,1},{5,3},{7,5},{8,14},{10,8},{12,... | collective-permute-start | bytes 983048 | tf_op jit(solution)/shard_map/ppermute | solution.py:36
  672.0 8.9 %collective-permute-start.38 = (bf16[256,640]{0,1:T(8,128)(2,1)S(1)}, bf16[256,640]{0,1:T(8,128)(2,1)S(1)}, u32[]{:S(2)}, u32[]{:S(2)}) collective-permute-start(bf16[256,640]{0,1:T(8,128)(2,1)S(1)} %get-tuple-element.44), channel_id=1, source_target_pairs={{0,4},{2,6},{4,0},{6,2},{1,5},{3,7},{5,1},{7,3},{8,12},{10,14},{12... | collective-permute-start | bytes 983048 | tf_op jit(solution)/shard_map/ppermute | solution.py:36
  672.7 17.3 %collective-permute-start.39 = (bf16[256,640]{0,1:T(8,128)(2,1)S(1)}, bf16[256,640]{0,1:T(8,128)(2,1)S(1)}, u32[]{:S(2)}, u32[]{:S(2)}) collective-permute-start(bf16[256,640]{0,1:T(8,128)(2,1)S(1)} %get-tuple-element.44), channel_id=1, source_target_pairs={{0,2},{2,4},{4,6},{6,0},{1,3},{3,5},{5,7},{7,1},{8,10},{10,12},{12... | collective-permute-start | bytes 983048 | tf_op jit(solution)/shard_map/ppermute | solution.py:36
  692.4 10.8 %collective-permute-start.40 = (bf16[2,256,640]{1,2,0:T(8,128)(2,1)}, bf16[2,256,640]{1,2,0:T(8,128)(2,1)}, u32[]{:S(2)}, u32[]{:S(2)}) collective-permute-start(bf16[2,256,640]{1,2,0:T(8,128)(2,1)} %constant_dynamic-slice_fusion.1), channel_id=1, source_target_pairs={{0,1},{1,0},{2,3},{3,2},{4,5},{5,4},{6,7},{7,6},{8,9},{9,8},{10,11... | collective-permute-start | bytes 1966088 | tf_op jit(solution)/shard_map/ppermute | solution.py:32
  (94 other events, 1312.5 us)
Sparse Core Ops, SparseCore 0:
  21.6 46.7 all-gather.4
  70.6 56.2 all-gather.10
  129.0 51.5 all-gather.8
  182.6 51.3 all-gather.6
  374.4 41.6 reduce-scatter.6
  456.0 44.1 reduce-scatter.8
  503.2 44.1 reduce-scatter.10
  602.5 46.9 reduce-scatter.4
where the time goes:
time: 734 us; the launch traced here: 725 us
  waiting for transfers between devices  310 us (42%)
  matrix products  114 us (16%)
  starting transfers between devices  91.1 us (12%)
  blocking collectives  70.6 us (10%)
  local copies, waits for them, and re-layouts  64.2 us (9%)
  other arithmetic  58.3 us (8%)
  between operations  17 us (2%)
    ppermute x36, waiting for transfers between devices, shift_x(): return lax.ppermute(value, 'x', [(i, (i + hop) % 4) for i in range(4)])  148 us
    psum x1, blocking collectives, per_device(): lax.psum(jnp.stack([gain_attn_local, gain_ffn_local]), ('yl', 'z', 'yh',...  70.6 us
    all_gather x3, waiting for transfers between devices, hidden_units(): own = lax.all_gather(own, SHARD, axis=0, tiled=True)  70.4 us
    ppermute x6, waiting for transfers between devices, across_y(): return lax.ppermute(value, 'yh', SWAP)  46.1 us
    ppermute x13, starting transfers between devices, swap_cores(): return lax.ppermute(value, 'tp', SWAP)  43.7 us
    all_gather x1, waiting for transfers between devices, per_device(): pack = lax.all_gather(pack, SHARD, axis=0, tiled=True)  42.6 us
    ppermute x36, starting transfers between devices, shift_x(): return lax.ppermute(value, 'x', [(i, (i + hop) % 4) for i in range(4)])  40.2 us
    unnamed x222, local copies, waits for them, and re-layouts  38.6 us
  transfers between devices with their start and end apart: 64, of which 31 were waited for; matrix products, arithmetic and copies ran while one was open for 26% of the time, Pallas kernels for 0%

commit v1 on v0

--- a/solution.py
+++ b/solution.py
@@ -1,3 +1,4 @@
+import functools
 import jax
 import jax.numpy as jnp
 from jax import lax
@@ -10,6 +11,13 @@
 BF16 = jnp.bfloat16
 SHARD = ("yl", "z")
 SWAP = ((0, 1), (1, 0))
+
+
+def zone_list(field, mesh_ax):
+    return jax.lax.all_gather(field, mesh_ax).sum(axis=0)
+
+
+link_the_ratios = functools.partial(zone_list, mesh_ax=("yl", "z", "yh", "x", "tp"))
 
 
 def half(value):
@@ -261,7 +269,7 @@
     )
     input_part, gain_attn_local = norm_backward(xval, root_attn, gain_attn, d_normed_attn)
     input_grad = both_cores(half(d_middle + input_part))
-    gains = lax.psum(jnp.stack([gain_attn_local, gain_ffn_local]), ("yl", "z", "yh", "x", "tp"))
+    gains = link_the_ratios(jnp.stack([gain_attn_local, gain_ffn_local]))
     owned = width // 8
     gains = lax.dynamic_slice_in_dim(
         gains, (lax.axis_index("yl") * 4 + lax.axis_index("z")) * owned, owned, axis=1

time: 734 us -> 882 us (1.20)
  waiting for transfers between devices: 310 us -> 533 us
  blocking collectives: 70.6 us -> 0 us
    all_gather x0 -> x1, waiting for transfers between devices: none -> 147 us  [zone_list(): return jax.lax.all_gather(field, mesh_ax).sum(axis=0)]
    reduce_scatter x4, waiting for transfers between devices: 0.03 us -> 90.5 us  [reduce_columns(): value = lax.psum_scatter(value, SHARD, scatter_dimension=0, tiled=True)]
    psum x1 -> x0, blocking collectives: 70.6 us -> none  [per_device(): lax.psum(jnp.stack([gain_attn_local, gain_ffn_local]), ('yl', 'z', 'yh',...]
    ppermute x6, waiting for transfers between devices: 46.1 us -> 18.5 us  [across_y(): return lax.ppermute(value, 'yh', SWAP)]
    ppermute x13, waiting for transfers between devices: 0.03 us -> 11.3 us  [swap_cores(): return lax.ppermute(value, 'tp', SWAP)]
    ppermute x36, waiting for transfers between devices: 148 us -> 157 us  [shift_x(): return lax.ppermute(value, 'x', [(i, (i + hop) % 4) for i in range(4)])]
    unnamed x222 -> x218, local copies, waits for them, and re-layouts: 38.6 us -> 34.7 us
  transfers between devices with their start and end apart: 64 -> 65, of which waited for: 31 -> 40; matrix products, arithmetic and copies ran while one was open for 26% -> 20% of each run, Pallas kernels for 0% -> 0%
where the time goes in v1:
time: 882 us; the launch traced here: 870 us
  waiting for transfers between devices  533 us (60%)
  matrix products  111 us (13%)
  starting transfers between devices  94.4 us (11%)
  other arithmetic  58.8 us (7%)
  local copies, waits for them, and re-layouts  56 us (6%)
  between operations  16.7 us (2%)
    ppermute x36, waiting for transfers between devices, shift_x(): return lax.ppermute(value, 'x', [(i, (i + hop) % 4) for i in range(4)])  157 us
    all_gather x1, waiting for transfers between devices, zone_list(): return jax.lax.all_gather(field, mesh_ax).sum(axis=0)  147 us
    reduce_scatter x4, waiting for transfers between devices, reduce_columns(): value = lax.psum_scatter(value, SHARD, scatter_dimension=0, tiled=True)  90.5 us
    all_gather x3, waiting for transfers between devices, hidden_units(): own = lax.all_gather(own, SHARD, axis=0, tiled=True)  63.2 us
    ppermute x36, starting transfers between devices, shift_x(): return lax.ppermute(value, 'x', [(i, (i + hop) % 4) for i in range(4)])  47 us
    all_gather x1, waiting for transfers between devices, per_device(): pack = lax.all_gather(pack, SHARD, axis=0, tiled=True)  42.6 us
    ppermute x13, starting transfers between devices, swap_cores(): return lax.ppermute(value, 'tp', SWAP)  41.2 us
    unnamed x218, local copies, waits for them, and re-layouts  34.7 us
  transfers between devices with their start and end apart: 65, of which 40 were waited for; matrix products, arithmetic and copies ran while one was open for 20% of the time, Pallas kernels for 0%

profile of v1, /device:TPU:17, one launch (start us, length us, event | category | flops | bytes accessed | tf_op | source)
XLA Modules:
  0.0 870.0 jit_solution(6439129017536875828)
XLA Ops:
  25.9 42.6 %all-gather.8.cloned.1.call-done = bf16[2048,640]{0,1:T(8,128)(2,1)} async-done(((bf16[256,640]{0,1:T(8,128)(2,1)}), bf16[2048,640]{0,1:T(8,128)(2,1)}) %all-gather.8.cloned.1.call-update) | async-done | bytes 2621456 | tf_op jit(solution)/shard_map/all_gather | solution.py:119
  68.4 4.7 collective-permute-start.4
  85.0 4.2 collective-permute-done.2
  89.2 12.2 %collective-permute-done.1 = bf16[128,2048]{1,0:T(8,128)(2,1)} collective-permute-done((bf16[128,2048]{1,0:T(8,128)(2,1)}, bf16[128,2048]{1,0:T(8,128)(2,1)}, u32[]{:S(2)}, u32[]{:S(2)}) %collective-permute-start.1) | collective-permute-done | bytes 524320 | tf_op jit(solution)/shard_map/ppermute | solution.py:44
  101.4 3.4 fusion.14
  108.1 12.3 %collective-permute-done.5 = bf16[512,256]{1,0:T(8,128)(2,1)S(1)} collective-permute-done((bf16[512,256]{1,0:T(8,128)(2,1)S(1)}, bf16[512,256]{1,0:T(8,128)(2,1)S(1)}, u32[]{:S(2)}, u32[]{:S(2)}) %collective-permute-start.5) | collective-permute-done | bytes 262176 | tf_op jit(solution)/shard_map/ppermute | solution.py:164
  124.2 2.6 all-gather.14.cloned.1.call-done
  126.8 5.7 collective-permute-start.15
  138.6 3.6 select_reduce_fusion
  142.2 5.0 fusion.1
  148.0 5.8 fusion.43
  153.8 3.3 fusion.129
  162.2 17.7 %all-gather.12.cloned.1.call-done = bf16[2048,704]{0,1:T(8,128)(2,1)} async-done(((bf16[256,704]{0,1:T(8,128)(2,1)}), bf16[2048,704]{0,1:T(8,128)(2,1)}) %all-gather.12.cloned.1.call-update) | async-done | bytes 2883600 | tf_op jit(solution)/shard_map/all_gather | solution.py:129
  179.9 5.0 collective-permute-start.14
  190.0 42.8 %all-gather.10.cloned.1.call-done = bf16[2048,704]{0,1:T(8,128)(2,1)} async-done(((bf16[256,704]{0,1:T(8,128)(2,1)}), bf16[2048,704]{0,1:T(8,128)(2,1)}) %all-gather.10.cloned.1.call-update) | async-done | bytes 2883600 | tf_op jit(solution)/shard_map/all_gather | solution.py:129
  232.8 5.1 collective-permute-start.13
  242.7 11.4 %collective-permute-done.20 = bf16[128,2048]{1,0:T(8,128)(2,1)S(1)} collective-permute-done((bf16[128,2048]{1,0:T(8,128)(2,1)}, bf16[128,2048]{1,0:T(8,128)(2,1)S(1)}, u32[]{:S(2)}, u32[]{:S(2)}) %collective-permute-start.20) | collective-permute-done | bytes 524320 | tf_op jit(solution)/shard_map/ppermute | solution.py:44
  257.5 4.0 fusion.104
  261.5 6.7 collective-permute-done.11
  268.3 12.2 %collective-permute-done.10 = bf16[128,2048]{1,0:T(8,128)(2,1)S(1)} collective-permute-done((bf16[128,2048]{1,0:T(8,128)(2,1)S(1)}, bf16[128,2048]{1,0:T(8,128)(2,1)S(1)}, u32[]{:S(2)}, u32[]{:S(2)}) %collective-permute-start.10) | collective-permute-done | bytes 524320 | tf_op jit(solution)/shard_map/ppermute | solution.py:44
  283.9 3.5 fusion.106
  287.5 3.7 multiply_convert_fusion.2
  293.5 3.6 multiply_convert_fusion.3
  300.9 4.1 fusion.112
  305.2 3.2 collective-permute-start.25
  311.7 3.8 fusion.130
  317.8 10.3 %collective-permute-done.25 = bf16[128,2048]{1,0:T(8,128)(2,1)S(1)} collective-permute-done((bf16[128,2048]{1,0:T(8,128)(2,1)S(1)}, bf16[128,2048]{1,0:T(8,128)(2,1)S(1)}, u32[]{:S(2)}, u32[]{:S(2)}) %collective-permute-start.25) | collective-permute-done | bytes 524320 | tf_op jit(solution)/shard_map/ppermute | solution.py:44
  328.1 4.1 collective-permute-done.23
  332.7 19.7 %collective-permute-done.18 = bf16[128,2048]{1,0:T(8,128)(2,1)S(1)} collective-permute-done((bf16[128,2048]{1,0:T(8,128)(2,1)S(1)}, bf16[128,2048]{1,0:T(8,128)(2,1)S(1)}, u32[]{:S(2)}, u32[]{:S(2)}) %collective-permute-start.18) | collective-permute-done | bytes 524320 | tf_op jit(solution)/shard_map/ppermute | solution.py:44
  360.5 3.3 convolution_convert_fusion.2
  363.8 2.8 collective-permute-start.41
  368.3 12.5 %collective-permute-done.27 = bf16[128,2048]{1,0:T(8,128)(2,1)S(1)} collective-permute-done((bf16[128,2048]{1,0:T(8,128)(2,1)S(1)}, bf16[128,2048]{1,0:T(8,128)(2,1)S(1)}, u32[]{:S(2)}, u32[]{:S(2)}) %collective-permute-start.27) | collective-permute-done | bytes 524320 | tf_op jit(solution)/shard_map/ppermute | solution.py:44
  384.2 12.5 %multiply_convert_fusion = bf16[4,512,2048]{2,1,0:T(8,128)(2,1)} fusion(f32[4,512,2048]{2,1,0:T(8,128)} %copy-done.8, f32[4,512]{1,0:T(4,128)S(1)} %get-tuple-element.171, f32[4,512]{1,0:T(4,128)S(1)} %log_add_fusion, pred[512,2048]{1,0:T(8,128)(4,1)S(1)} %copy-done.17, bf16[4,512,128]{1,2,0:T(8,128)(2,1)S(1)} %bitcast.248, bf16[2048,256]{1,0:T(8,128)(2,1)S(1)} %copy-done.41), kind=kOutput, calls=%fused_computation | convolution fusion | flops 1103101952 | bytes 27279360 | tf_op jit(solution)/shard_map/htd,nd->htn/dot_general | solution.py:239
  396.8 5.9 convolution_bitcast_fusion
  402.6 8.1 fusion.9
  414.2 3.0 add_convert_fusion.2
  419.9 6.0 fusion.46
  425.9 4.7 collective-permute-done.30
  438.9 8.7 %collective-permute-done.33 = bf16[128,2048]{1,0:T(8,128)(2,1)S(1)} collective-permute-done((bf16[128,2048]{1,0:T(8,128)(2,1)S(1)}, bf16[128,2048]{1,0:T(8,128)(2,1)S(1)}, u32[]{:S(2)}, u32[]{:S(2)}) %collective-permute-start.33) | collective-permute-done | bytes 524320 | tf_op jit(solution)/shard_map/ppermute | solution.py:44
  447.6 3.9 collective-permute-done.32
  451.5 9.0 %collective-permute-done.31 = bf16[128,2048]{1,0:T(8,128)(2,1)S(1)} collective-permute-done((bf16[128,2048]{1,0:T(8,128)(2,1)S(1)}, bf16[128,2048]{1,0:T(8,128)(2,1)S(1)}, u32[]{:S(2)}, u32[]{:S(2)}) %collective-permute-start.31) | collective-permute-done | bytes 524320 | tf_op jit(solution)/shard_map/ppermute | solution.py:44
  462.7 2.8 convolution_convert_fusion.1
  465.5 4.0 collective-permute-start.46
  469.5 4.9 collective-permute-done.46
  474.4 3.0 add_convert_fusion.1
  478.7 3.0 convolution_convert_fusion
  482.4 4.9 collective-permute-done.51
  487.3 4.7 add_convert_fusion
  496.0 4.9 fusion.48
  501.6 2.6 select_convert_fusion
  511.2 4.1 add_convert_fusion.3
  517.7 147.3 %all-gather.16.cloned.1.call-done = f32[128,2,2048]{2,1,0:T(2,128)} async-done(((f32[1,2,2048]{2,1,0:T(2,128)}), f32[128,2,2048]{2,1,0:T(2,128)}) %all-gather.16.cloned.1.call-update) | async-done | bytes 2097168 | tf_op jit(solution)/shard_map/all_gather | solution.py:17
  667.1 42.0 %reduce-scatter.9.cloned.1.call-done = bf16[256,704]{0,1:T(8,128)(2,1)} async-done(((bf16[2048,704]{0,1:T(8,128)(2,1)}), bf16[256,704]{0,1:T(8,128)(2,1)}) %reduce-scatter.9.cloned.1.call-update) | async-done | bytes 360464 | tf_op jit(solution)/shard_map/reduce_scatter | solution.py:221
  710.2 46.5 %reduce-scatter.11.cloned.1.call-done = bf16[256,704]{0,1:T(8,128)(2,1)} async-done(((bf16[2048,704]{0,1:T(8,128)(2,1)}), bf16[256,704]{0,1:T(8,128)(2,1)}) %reduce-scatter.11.cloned.1.call-update) | async-done | bytes 360464 | tf_op jit(solution)/shard_map/reduce_scatter | solution.py:221
  764.7 2.7 collective-permute-start.49
  768.8 3.9 collective-permute-start.53
  772.7 8.4 collective-permute-done.45
  781.2 2.6 collective-permute-done.48
  784.0 11.5 %collective-permute-done.50 = bf16[256,704]{0,1:T(8,128)(2,1)S(1)} collective-permute-done((bf16[256,704]{0,1:T(8,128)(2,1)S(1)}, bf16[256,704]{0,1:T(8,128)(2,1)S(1)}, u32[]{:S(2)}, u32[]{:S(2)}) %collective-permute-start.50) | collective-permute-done | bytes 360480 | tf_op jit(solution)/shard_map/ppermute | solution.py:44
  804.1 3.8 collective-permute-done.55
  817.6 3.7 collective-permute-done.37
  823.1 3.4 collective-permute-done.39
  828.9 9.7 %collective-permute-start.40 = (bf16[2,256,640]{1,2,0:T(8,128)(2,1)}, bf16[2,256,640]{1,2,0:T(8,128)(2,1)}, u32[]{:S(2)}, u32[]{:S(2)}) collective-permute-start(bf16[2,256,640]{1,2,0:T(8,128)(2,1)} %constant_dynamic-slice_fusion.1), channel_id=1, source_target_pairs={{0,1},{1,0},{2,3},{3,2},{4,5},{5,4},{6,7},{7,6},{8,9},{9,8},{10,11... | collective-permute-start | bytes 1966088 | tf_op jit(solution)/shard_map/ppermute | solution.py:40
  841.5 3.4 copy.68
  (444 shorter events, 179.1 us)
Async XLA Ops:
  7.2 61.2 %all-gather.8.cloned.1.call-start = ((), (), s32[]{:S(2)}) async-start(), calls=%async_computation.4 | async-start | bytes 2949120 | tf_op jit(solution)/shard_map/all_gather | solution.py:119
  15.8 3.9 collective-permute-start.3
  21.5 105.3 %all-gather.14.cloned.1.call-start = ((), (), s32[]{:S(2)}) async-start(), calls=%async_computation.7 | async-start | bytes 3244032 | tf_op jit(solution)/shard_map/all_gather | solution.py:129
  22.7 157.2 %all-gather.12.cloned.1.call-start = ((), (), s32[]{:S(2)}) async-start(), calls=%async_computation.6 | async-start | bytes 3244032 | tf_op jit(solution)/shard_map/all_gather | solution.py:129
  25.1 207.8 %all-gather.10.cloned.1.call-start = ((), (), s32[]{:S(2)}) async-start(), calls=%async_computation.5 | async-start | bytes 3244032 | tf_op jit(solution)/shard_map/all_gather | solution.py:129
  68.4 14.2 %collective-permute-start.4 = (bf16[2048,640]{0,1:T(8,128)(2,1)}, bf16[2048,640]{0,1:T(8,128)(2,1)}, u32[]{:S(2)}, u32[]{:S(2)}) collective-permute-start(bf16[2048,640]{0,1:T(8,128)(2,1)} %all-gather.8.cloned.1.call-done), channel_id=1, source_target_pairs={{0,1},{1,0},{2,3},{3,2},{4,5},{5,4},{6,7},{7,6},{8,9},{9,8},{10,11... | collective-permute-start | bytes 7864328 | tf_op jit(solution)/shard_map/ppermute | solution.py:40
  74.1 15.1 %collective-permute-start.2 = (bf16[128,2048]{1,0:T(8,128)(2,1)}, bf16[128,2048]{1,0:T(8,128)(2,1)}, u32[]{:S(2)}, u32[]{:S(2)}) collective-permute-start(bf16[128,2048]{1,0:T(8,128)(2,1)} %fusion.23), channel_id=1, source_target_pairs={{0,2},{2,4},{4,6},{6,0},{1,3},{3,5},{5,7},{7,1},{8,10},{10,12},{12... | collective-permute-start | bytes 1572872 | tf_op jit(solution)/shard_map/ppermute | solution.py:44
  75.3 26.0 %collective-permute-start.1 = (bf16[128,2048]{1,0:T(8,128)(2,1)}, bf16[128,2048]{1,0:T(8,128)(2,1)}, u32[]{:S(2)}, u32[]{:S(2)}) collective-permute-start(bf16[128,2048]{1,0:T(8,128)(2,1)} %fusion.23), channel_id=1, source_target_pairs={{0,4},{2,6},{4,0},{6,2},{1,5},{3,7},{5,1},{7,3},{8,12},{10,14},{12... | collective-permute-start | bytes 1572872 | tf_op jit(solution)/shard_map/ppermute | solution.py:44
  77.7 23.6 %collective-permute-start = (bf16[128,2048]{1,0:T(8,128)(2,1)}, bf16[128,2048]{1,0:T(8,128)(2,1)}, u32[]{:S(2)}, u32[]{:S(2)}) collective-permute-start(bf16[128,2048]{1,0:T(8,128)(2,1)} %fusion.23), channel_id=1, source_target_pairs={{0,6},{2,0},{4,2},{6,4},{1,7},{3,1},{5,3},{7,5},{8,14},{10,8},{12,... | collective-permute-start | bytes 1572872 | tf_op jit(solution)/shard_map/ppermute | solution.py:44
  81.2 434.2 %reduce-scatter.7.cloned.1.call-start = ((), (), s32[]{:S(2)}) async-start(), calls=%async_computation.9 | async-start | bytes 3244032 | tf_op jit(solution)/shard_map/reduce_scatter | solution.py:221
  106.8 13.6 %collective-permute-start.5 = (bf16[512,256]{1,0:T(8,128)(2,1)S(1)}, bf16[512,256]{1,0:T(8,128)(2,1)S(1)}, u32[]{:S(2)}, u32[]{:S(2)}) collective-permute-start(bf16[512,256]{1,0:T(8,128)(2,1)S(1)} %pad_maximum_fusion.29), channel_id=1, source_target_pairs={{0,8},{8,0},{1,9},{9,1},{2,10},{10,2},{3,11},{11,3},{4,12},{12,4},... | collective-permute-start | bytes 786440 | tf_op jit(solution)/shard_map/ppermute | solution.py:164
  121.3 16.1 %collective-permute-start.6 = (bf16[1024,256]{1,0:T(8,128)(2,1)}, bf16[1024,256]{1,0:T(8,128)(2,1)}, u32[]{:S(2)}, u32[]{:S(2)}) collective-permute-start(bf16[1024,256]{1,0:T(8,128)(2,1)} %pad_maximum_fusion.19), channel_id=1, source_target_pairs={{0,1},{1,0},{2,3},{3,2},{4,5},{5,4},{6,7},{7,6},{8,9},{9,8},{10,11... | collective-permute-start | bytes 1572872 | tf_op jit(solution)/shard_map/ppermute | solution.py:40
  126.8 129.6 %collective-permute-start.15 = (bf16[2048,704]{0,1:T(8,128)(2,1)}, bf16[2048,704]{0,1:T(8,128)(2,1)}, u32[]{:S(2)}, u32[]{:S(2)}) collective-permute-start(bf16[2048,704]{0,1:T(8,128)(2,1)} %all-gather.14.cloned.1.call-done), channel_id=1, source_target_pairs={{0,1},{1,0},{2,3},{3,2},{4,5},{5,4},{6,7},{7,6},{8,9},{9,8},{10,11... | collective-permute-start | bytes 8650760 | tf_op jit(solution)/shard_map/ppermute | solution.py:40
  158.3 28.5 %collective-permute-start.9 = (bf16[128,2048]{1,0:T(8,128)(2,1)}, bf16[128,2048]{1,0:T(8,128)(2,1)S(1)}, u32[]{:S(2)}, u32[]{:S(2)}) collective-permute-start(bf16[128,2048]{1,0:T(8,128)(2,1)} %get-tuple-element.91), channel_id=1, source_target_pairs={{0,6},{2,0},{4,2},{6,4},{1,7},{3,1},{5,3},{7,5},{8,14},{10,8},{12,... | collective-permute-start | bytes 1572872 | tf_op jit(solution)/shard_map/ppermute | solution.py:44
  160.4 27.6 %collective-permute-start.8 = (bf16[128,2048]{1,0:T(8,128)(2,1)}, bf16[128,2048]{1,0:T(8,128)(2,1)}, u32[]{:S(2)}, u32[]{:S(2)}) collective-permute-start(bf16[128,2048]{1,0:T(8,128)(2,1)} %get-tuple-element.92), channel_id=1, source_target_pairs={{0,2},{2,4},{4,6},{6,0},{1,3},{3,5},{5,7},{7,1},{8,10},{10,12},{12... | collective-permute-start | bytes 1572872 | tf_op jit(solution)/shard_map/ppermute | solution.py:44
  160.4 72.5 %collective-permute-start.7 = (bf16[128,2048]{1,0:T(8,128)(2,1)}, bf16[128,2048]{1,0:T(8,128)(2,1)}, u32[]{:S(2)}, u32[]{:S(2)}) collective-permute-start(bf16[128,2048]{1,0:T(8,128)(2,1)} %get-tuple-element.90), channel_id=1, source_target_pairs={{0,4},{2,6},{4,0},{6,2},{1,5},{3,7},{5,1},{7,3},{8,12},{10,14},{12... | collective-permute-start | bytes 1572872 | tf_op jit(solution)/shard_map/ppermute | solution.py:44
  179.9 104.0 %collective-permute-start.14 = (bf16[2048,704]{0,1:T(8,128)(2,1)}, bf16[2048,704]{0,1:T(8,128)(2,1)}, u32[]{:S(2)}, u32[]{:S(2)}) collective-permute-start(bf16[2048,704]{0,1:T(8,128)(2,1)} %all-gather.12.cloned.1.call-done), channel_id=1, source_target_pairs={{0,1},{1,0},{2,3},{3,2},{4,5},{5,4},{6,7},{7,6},{8,9},{9,8},{10,11... | collective-permute-start | bytes 8650760 | tf_op jit(solution)/shard_map/ppermute | solution.py:40
  186.9 53.1 %collective-permute-start.22 = (bf16[128,2048]{1,0:T(8,128)(2,1)}, bf16[128,2048]{1,0:T(8,128)(2,1)}, u32[]{:S(2)}, u32[]{:S(2)}) collective-permute-start(bf16[128,2048]{1,0:T(8,128)(2,1)} %fusion.20), channel_id=1, source_target_pairs={{0,2},{2,4},{4,6},{6,0},{1,3},{3,5},{5,7},{7,1},{8,10},{10,12},{12... | collective-permute-start | bytes 1572872 | tf_op jit(solution)/shard_map/ppermute | solution.py:44
  187.9 54.7 %collective-permute-start.21 = (bf16[128,2048]{1,0:T(8,128)(2,1)}, bf16[128,2048]{1,0:T(8,128)(2,1)}, u32[]{:S(2)}, u32[]{:S(2)}) collective-permute-start(bf16[128,2048]{1,0:T(8,128)(2,1)} %fusion.20), channel_id=1, source_target_pairs={{0,4},{2,6},{4,0},{6,2},{1,5},{3,7},{5,1},{7,3},{8,12},{10,14},{12... | collective-permute-start | bytes 1572872 | tf_op jit(solution)/shard_map/ppermute | solution.py:44
  232.8 54.6 %collective-permute-start.13 = (bf16[2048,704]{0,1:T(8,128)(2,1)}, bf16[2048,704]{0,1:T(8,128)(2,1)S(1)}, u32[]{:S(2)}, u32[]{:S(2)}) collective-permute-start(bf16[2048,704]{0,1:T(8,128)(2,1)} %all-gather.10.cloned.1.call-done), channel_id=1, source_target_pairs={{0,1},{1,0},{2,3},{3,2},{4,5},{5,4},{6,7},{7,6},{8,9},{9,8},{10,11... | collective-permute-start | bytes 8650760 | tf_op jit(solution)/shard_map/ppermute | solution.py:40
  240.0 14.1 %collective-permute-start.20 = (bf16[128,2048]{1,0:T(8,128)(2,1)}, bf16[128,2048]{1,0:T(8,128)(2,1)S(1)}, u32[]{:S(2)}, u32[]{:S(2)}) collective-permute-start(bf16[128,2048]{1,0:T(8,128)(2,1)} %fusion.20), channel_id=1, source_target_pairs={{0,6},{2,0},{4,2},{6,4},{1,7},{3,1},{5,3},{7,5},{8,14},{10,8},{12,... | collective-permute-start | bytes 1572872 | tf_op jit(solution)/shard_map/ppermute | solution.py:44
  242.7 18.8 %collective-permute-start.12 = (bf16[128,2048]{1,0:T(8,128)(2,1)S(1)}, bf16[128,2048]{1,0:T(8,128)(2,1)S(1)}, u32[]{:S(2)}, u32[]{:S(2)}) collective-permute-start(bf16[128,2048]{1,0:T(8,128)(2,1)S(1)} %multiply_convert_fusion.8), channel_id=1, source_target_pairs={{0,2},{2,4},{4,6},{6,0},{1,3},{3,5},{5,7},{7,1},{8,10},{10,12},{12... | collective-permute-start | bytes 1572872 | tf_op jit(solution)/shard_map/ppermute | solution.py:44
  254.1 14.1 %collective-permute-start.11 = (bf16[128,2048]{1,0:T(8,128)(2,1)S(1)}, bf16[128,2048]{1,0:T(8,128)(2,1)S(1)}, u32[]{:S(2)}, u32[]{:S(2)}) collective-permute-start(bf16[128,2048]{1,0:T(8,128)(2,1)S(1)} %multiply_convert_fusion.8), channel_id=1, source_target_pairs={{0,4},{2,6},{4,0},{6,2},{1,5},{3,7},{5,1},{7,3},{8,12},{10,14},{12... | collective-permute-start | bytes 1572872 | tf_op jit(solution)/shard_map/ppermute | solution.py:44
  256.5 24.0 %collective-permute-start.10 = (bf16[128,2048]{1,0:T(8,128)(2,1)S(1)}, bf16[128,2048]{1,0:T(8,128)(2,1)S(1)}, u32[]{:S(2)}, u32[]{:S(2)}) collective-permute-start(bf16[128,2048]{1,0:T(8,128)(2,1)S(1)} %multiply_convert_fusion.8), channel_id=1, source_target_pairs={{0,6},{2,0},{4,2},{6,4},{1,7},{3,1},{5,3},{7,5},{8,14},{10,8},{12,... | collective-permute-start | bytes 1572872 | tf_op jit(solution)/shard_map/ppermute | solution.py:44
  305.2 22.9 %collective-permute-start.25 = (bf16[128,2048]{1,0:T(8,128)(2,1)S(1)}, bf16[128,2048]{1,0:T(8,128)(2,1)S(1)}, u32[]{:S(2)}, u32[]{:S(2)}) collective-permute-start(bf16[128,2048]{1,0:T(8,128)(2,1)S(1)} %get-tuple-element.85), channel_id=1, source_target_pairs={{0,6},{2,0},{4,2},{6,4},{1,7},{3,1},{5,3},{7,5},{8,14},{10,8},{12,... | collective-permute-start | bytes 1572872 | tf_op jit(solution)/shard_map/ppermute | solution.py:44
  308.3 19.8 %collective-permute-start.24 = (bf16[128,2048]{1,0:T(8,128)(2,1)S(1)}, bf16[128,2048]{1,0:T(8,128)(2,1)S(1)}, u32[]{:S(2)}, u32[]{:S(2)}) collective-permute-start(bf16[128,2048]{1,0:T(8,128)(2,1)S(1)} %get-tuple-element.86), channel_id=1, source_target_pairs={{0,2},{2,4},{4,6},{6,0},{1,3},{3,5},{5,7},{7,1},{8,10},{10,12},{12... | collective-permute-start | bytes 1572872 | tf_op jit(solution)/shard_map/ppermute | solution.py:44
  308.3 23.8 %collective-permute-start.23 = (bf16[128,2048]{1,0:T(8,128)(2,1)S(1)}, bf16[128,2048]{1,0:T(8,128)(2,1)S(1)}, u32[]{:S(2)}, u32[]{:S(2)}) collective-permute-start(bf16[128,2048]{1,0:T(8,128)(2,1)S(1)} %get-tuple-element.84), channel_id=1, source_target_pairs={{0,4},{2,6},{4,0},{6,2},{1,5},{3,7},{5,1},{7,3},{8,12},{10,14},{12... | collective-permute-start | bytes 1572872 | tf_op jit(solution)/shard_map/ppermute | solution.py:44
  315.6 36.8 %collective-permute-start.18 = (bf16[128,2048]{1,0:T(8,128)(2,1)S(1)}, bf16[128,2048]{1,0:T(8,128)(2,1)S(1)}, u32[]{:S(2)}, u32[]{:S(2)}) collective-permute-start(bf16[128,2048]{1,0:T(8,128)(2,1)S(1)} %get-tuple-element.88), channel_id=1, source_target_pairs={{0,6},{2,0},{4,2},{6,4},{1,7},{3,1},{5,3},{7,5},{8,14},{10,8},{12,... | collective-permute-start | bytes 1572872 | tf_op jit(solution)/shard_map/ppermute | solution.py:44
  317.2 35.3 %collective-permute-start.17 = (bf16[128,2048]{1,0:T(8,128)(2,1)S(1)}, bf16[128,2048]{1,0:T(8,128)(2,1)S(1)}, u32[]{:S(2)}, u32[]{:S(2)}) collective-permute-start(bf16[128,2048]{1,0:T(8,128)(2,1)S(1)} %get-tuple-element.89), channel_id=1, source_target_pairs={{0,2},{2,4},{4,6},{6,0},{1,3},{3,5},{5,7},{7,1},{8,10},{10,12},{12... | collective-permute-start | bytes 1572872 | tf_op jit(solution)/shard_map/ppermute | solution.py:44
  328.1 26.6 %collective-permute-start.16 = (bf16[128,2048]{1,0:T(8,128)(2,1)S(1)}, bf16[128,2048]{1,0:T(8,128)(2,1)S(1)}, u32[]{:S(2)}, u32[]{:S(2)}) collective-permute-start(bf16[128,2048]{1,0:T(8,128)(2,1)S(1)} %get-tuple-element.87), channel_id=1, source_target_pairs={{0,4},{2,6},{4,0},{6,2},{1,5},{3,7},{5,1},{7,3},{8,12},{10,14},{12... | collective-permute-start | bytes 1572872 | tf_op jit(solution)/shard_map/ppermute | solution.py:44
  356.6 11.7 %collective-permute-start.28 = (bf16[128,2048]{1,0:T(8,128)(2,1)S(1)}, bf16[128,2048]{1,0:T(8,128)(2,1)S(1)}, u32[]{:S(2)}, u32[]{:S(2)}) collective-permute-start(bf16[128,2048]{1,0:T(8,128)(2,1)S(1)} %get-tuple-element.46), channel_id=1, source_target_pairs={{0,2},{2,4},{4,6},{6,0},{1,3},{3,5},{5,7},{7,1},{8,10},{10,12},{12... | collective-permute-start | bytes 1572872 | tf_op jit(solution)/shard_map/ppermute | solution.py:44
  356.6 24.2 %collective-permute-start.27 = (bf16[128,2048]{1,0:T(8,128)(2,1)S(1)}, bf16[128,2048]{1,0:T(8,128)(2,1)S(1)}, u32[]{:S(2)}, u32[]{:S(2)}) collective-permute-start(bf16[128,2048]{1,0:T(8,128)(2,1)S(1)} %get-tuple-element.46), channel_id=1, source_target_pairs={{0,4},{2,6},{4,0},{6,2},{1,5},{3,7},{5,1},{7,3},{8,12},{10,14},{12... | collective-permute-start | bytes 1572872 | tf_op jit(solution)/shard_map/ppermute | solution.py:44
  359.2 23.3 %collective-permute-start.26 = (bf16[128,2048]{1,0:T(8,128)(2,1)S(1)}, bf16[128,2048]{1,0:T(8,128)(2,1)S(1)}, u32[]{:S(2)}, u32[]{:S(2)}) collective-permute-start(bf16[128,2048]{1,0:T(8,128)(2,1)S(1)} %get-tuple-element.46), channel_id=1, source_target_pairs={{0,6},{2,0},{4,2},{6,4},{1,7},{3,1},{5,3},{7,5},{8,14},{10,8},{12,... | collective-permute-start | bytes 1572872 | tf_op jit(solution)/shard_map/ppermute | solution.py:44
  363.8 50.4 %collective-permute-start.41 = (bf16[2048,704]{0,1:T(8,128)(2,1)}, bf16[2048,704]{0,1:T(8,128)(2,1)S(1)}, u32[]{:S(2)}, u32[]{:S(2)}) collective-permute-start(bf16[2048,704]{0,1:T(8,128)(2,1)} %convolution_convert_fusion.2), channel_id=1, source_target_pairs={{0,1},{1,0},{2,3},{3,2},{4,5},{5,4},{6,7},{7,6},{8,9},{9,8},{10,11... | collective-permute-start | bytes 8650760 | tf_op jit(solution)/shard_map/ppermute | solution.py:40
  411.7 5.5 collective-permute-start.29
  417.2 247.7 %all-gather.16.cloned.1.call-start = ((), (), s32[]{:S(2)}) async-start(), calls=%async_computation.12 | async-start | bytes 2113536 | tf_op jit(solution)/shard_map/all_gather | solution.py:17
  419.4 11.2 %collective-permute-start.30 = (bf16[512,256]{1,0:T(8,128)(2,1)S(1)}, bf16[512,256]{1,0:T(8,128)(2,1)S(1)}, u32[]{:S(2)}, u32[]{:S(2)}) collective-permute-start(bf16[512,256]{1,0:T(8,128)(2,1)S(1)} %slice.636), channel_id=1, source_target_pairs={{0,8},{8,0},{1,9},{9,1},{2,10},{10,2},{3,11},{11,3},{4,12},{12,4},... | collective-permute-start | bytes 786440 | tf_op jit(solution)/shard_map/ppermute | solution.py:164
  435.6 12.0 %collective-permute-start.33 = (bf16[128,2048]{1,0:T(8,128)(2,1)S(1)}, bf16[128,2048]{1,0:T(8,128)(2,1)S(1)}, u32[]{:S(2)}, u32[]{:S(2)}) collective-permute-start(bf16[128,2048]{1,0:T(8,128)(2,1)S(1)} %get-tuple-element.80), channel_id=1, source_target_pairs={{0,6},{2,0},{4,2},{6,4},{1,7},{3,1},{5,3},{7,5},{8,14},{10,8},{12,... | collective-permute-start | bytes 1572872 | tf_op jit(solution)/shard_map/ppermute | solution.py:44
  437.7 13.8 %collective-permute-start.32 = (bf16[128,2048]{1,0:T(8,128)(2,1)S(1)}, bf16[128,2048]{1,0:T(8,128)(2,1)S(1)}, u32[]{:S(2)}, u32[]{:S(2)}) collective-permute-start(bf16[128,2048]{1,0:T(8,128)(2,1)S(1)} %get-tuple-element.81), channel_id=1, source_target_pairs={{0,2},{2,4},{4,6},{6,0},{1,3},{3,5},{5,7},{7,1},{8,10},{10,12},{12... | collective-permute-start | bytes 1572872 | tf_op jit(solution)/shard_map/ppermute | solution.py:44
  437.7 22.9 %collective-permute-start.31 = (bf16[128,2048]{1,0:T(8,128)(2,1)S(1)}, bf16[128,2048]{1,0:T(8,128)(2,1)S(1)}, u32[]{:S(2)}, u32[]{:S(2)}) collective-permute-start(bf16[128,2048]{1,0:T(8,128)(2,1)S(1)} %get-tuple-element.79), channel_id=1, source_target_pairs={{0,4},{2,6},{4,0},{6,2},{1,5},{3,7},{5,1},{7,3},{8,12},{10,14},{12... | collective-permute-start | bytes 1572872 | tf_op jit(solution)/shard_map/ppermute | solution.py:44
  462.6 246.6 %reduce-scatter.9.cloned.1.call-start = ((), (), s32[]{:S(2)}) async-start(), calls=%async_computation.10 | async-start | bytes 3244032 | tf_op jit(solution)/shard_map/reduce_scatter | solution.py:221
  465.5 8.9 %collective-permute-start.46 = (bf16[2048,704]{0,1:T(8,128)(2,1)S(1)}, bf16[2048,704]{0,1:T(8,128)(2,1)S(1)}, u32[]{:S(2)}, u32[]{:S(2)}) collective-permute-start(bf16[2048,704]{0,1:T(8,128)(2,1)S(1)} %convolution_convert_fusion.1), channel_id=1, source_target_pairs={{0,1},{1,0},{2,3},{3,2},{4,5},{5,4},{6,7},{7,6},{8,9},{9,8},{10,11... | collective-permute-start | bytes 8650760 | tf_op jit(solution)/shard_map/ppermute | solution.py:40
  477.4 279.3 %reduce-scatter.11.cloned.1.call-start = ((), (), s32[]{:S(2)}) async-start(), calls=%async_computation.11 | async-start | bytes 3244032 | tf_op jit(solution)/shard_map/reduce_scatter | solution.py:221
  481.7 5.6 collective-permute-start.51
  492.0 310.7 %reduce-scatter.5.cloned.1.call-start = ((), (), s32[]{:S(2)}) async-start(), calls=%async_computation.8 | async-start | bytes 2949120 | tf_op jit(solution)/shard_map/reduce_scatter | solution.py:221
  504.2 7.0 collective-permute-start.35
  504.6 4.2 collective-permute-start.19
  515.4 241.9 %collective-permute-start.42 = (bf16[256,704]{0,1:T(8,128)(2,1)}, bf16[256,704]{0,1:T(8,128)(2,1)S(1)}, u32[]{:S(2)}, u32[]{:S(2)}) collective-permute-start(bf16[256,704]{0,1:T(8,128)(2,1)} %reduce-scatter.7.cloned.1.call-done), channel_id=1, source_target_pairs={{0,8},{8,0},{1,9},{9,1},{2,10},{10,2},{3,11},{11,3},{4,12},{12,4},... | collective-permute-start | bytes 1081352 | tf_op jit(solution)/shard_map/ppermute | solution.py:164
  709.1 51.8 %collective-permute-start.47 = (bf16[256,704]{0,1:T(8,128)(2,1)}, bf16[256,704]{0,1:T(8,128)(2,1)S(1)}, u32[]{:S(2)}, u32[]{:S(2)}) collective-permute-start(bf16[256,704]{0,1:T(8,128)(2,1)} %reduce-scatter.9.cloned.1.call-done), channel_id=1, source_target_pairs={{0,8},{8,0},{1,9},{9,1},{2,10},{10,2},{3,11},{11,3},{4,12},{12,4},... | collective-permute-start | bytes 1081352 | tf_op jit(solution)/shard_map/ppermute | solution.py:164
  756.7 8.0 collective-permute-start.52
  757.4 11.0 %collective-permute-start.43 = (bf16[256,704]{0,1:T(8,128)(2,1)S(1)}, bf16[256,704]{0,1:T(8,128)(2,1)S(1)}, u32[]{:S(2)}, u32[]{:S(2)}) collective-permute-start(bf16[256,704]{0,1:T(8,128)(2,1)S(1)} %get-tuple-element.42), channel_id=1, source_target_pairs={{0,6},{2,0},{4,2},{6,4},{1,7},{3,1},{5,3},{7,5},{8,14},{10,8},{12,... | collective-permute-start | bytes 1081352 | tf_op jit(solution)/shard_map/ppermute | solution.py:44
  759.9 8.9 %collective-permute-start.44 = (bf16[256,704]{0,1:T(8,128)(2,1)S(1)}, bf16[256,704]{0,1:T(8,128)(2,1)S(1)}, u32[]{:S(2)}, u32[]{:S(2)}) collective-permute-start(bf16[256,704]{0,1:T(8,128)(2,1)S(1)} %get-tuple-element.42), channel_id=1, source_target_pairs={{0,4},{2,6},{4,0},{6,2},{1,5},{3,7},{5,1},{7,3},{8,12},{10,14},{12... | collective-permute-start | bytes 1081352 | tf_op jit(solution)/shard_map/ppermute | solution.py:44
  760.4 20.7 %collective-permute-start.45 = (bf16[256,704]{0,1:T(8,128)(2,1)S(1)}, bf16[256,704]{0,1:T(8,128)(2,1)S(1)}, u32[]{:S(2)}, u32[]{:S(2)}) collective-permute-start(bf16[256,704]{0,1:T(8,128)(2,1)S(1)} %get-tuple-element.42), channel_id=1, source_target_pairs={{0,2},{2,4},{4,6},{6,0},{1,3},{3,5},{5,7},{7,1},{8,10},{10,12},{12... | collective-permute-start | bytes 1081352 | tf_op jit(solution)/shard_map/ppermute | solution.py:44
  762.1 21.7 %collective-permute-start.48 = (bf16[256,704]{0,1:T(8,128)(2,1)S(1)}, bf16[256,704]{0,1:T(8,128)(2,1)S(1)}, u32[]{:S(2)}, u32[]{:S(2)}) collective-permute-start(bf16[256,704]{0,1:T(8,128)(2,1)S(1)} %get-tuple-element.40), channel_id=1, source_target_pairs={{0,6},{2,0},{4,2},{6,4},{1,7},{3,1},{5,3},{7,5},{8,14},{10,8},{12,... | collective-permute-start | bytes 1081352 | tf_op jit(solution)/shard_map/ppermute | solution.py:44
  764.7 19.2 %collective-permute-start.49 = (bf16[256,704]{0,1:T(8,128)(2,1)S(1)}, bf16[256,704]{0,1:T(8,128)(2,1)S(1)}, u32[]{:S(2)}, u32[]{:S(2)}) collective-permute-start(bf16[256,704]{0,1:T(8,128)(2,1)S(1)} %get-tuple-element.40), channel_id=1, source_target_pairs={{0,4},{2,6},{4,0},{6,2},{1,5},{3,7},{5,1},{7,3},{8,12},{10,14},{12... | collective-permute-start | bytes 1081352 | tf_op jit(solution)/shard_map/ppermute | solution.py:44
  768.4 27.1 %collective-permute-start.50 = (bf16[256,704]{0,1:T(8,128)(2,1)S(1)}, bf16[256,704]{0,1:T(8,128)(2,1)S(1)}, u32[]{:S(2)}, u32[]{:S(2)}) collective-permute-start(bf16[256,704]{0,1:T(8,128)(2,1)S(1)} %get-tuple-element.40), channel_id=1, source_target_pairs={{0,2},{2,4},{4,6},{6,0},{1,3},{3,5},{5,7},{7,1},{8,10},{10,12},{12... | collective-permute-start | bytes 1081352 | tf_op jit(solution)/shard_map/ppermute | solution.py:44
  768.8 30.5 %collective-permute-start.53 = (bf16[256,704]{0,1:T(8,128)(2,1)}, bf16[256,704]{0,1:T(8,128)(2,1)S(1)}, u32[]{:S(2)}, u32[]{:S(2)}) collective-permute-start(bf16[256,704]{0,1:T(8,128)(2,1)} %get-tuple-element.38), channel_id=1, source_target_pairs={{0,6},{2,0},{4,2},{6,4},{1,7},{3,1},{5,3},{7,5},{8,14},{10,8},{12,... | collective-permute-start | bytes 1081352 | tf_op jit(solution)/shard_map/ppermute | solution.py:44
  781.1 22.3 %collective-permute-start.54 = (bf16[256,704]{0,1:T(8,128)(2,1)}, bf16[256,704]{0,1:T(8,128)(2,1)S(1)}, u32[]{:S(2)}, u32[]{:S(2)}) collective-permute-start(bf16[256,704]{0,1:T(8,128)(2,1)} %get-tuple-element.38), channel_id=1, source_target_pairs={{0,4},{2,6},{4,0},{6,2},{1,5},{3,7},{5,1},{7,3},{8,12},{10,14},{12... | collective-permute-start | bytes 1081352 | tf_op jit(solution)/shard_map/ppermute | solution.py:44
  783.8 24.1 %collective-permute-start.55 = (bf16[256,704]{0,1:T(8,128)(2,1)}, bf16[256,704]{0,1:T(8,128)(2,1)}, u32[]{:S(2)}, u32[]{:S(2)}) collective-permute-start(bf16[256,704]{0,1:T(8,128)(2,1)} %get-tuple-element.38), channel_id=1, source_target_pairs={{0,2},{2,4},{4,6},{6,0},{1,3},{3,5},{5,7},{7,1},{8,10},{10,12},{12... | collective-permute-start | bytes 1081352 | tf_op jit(solution)/shard_map/ppermute | solution.py:44
  802.7 7.9 collective-permute-start.36
  811.7 9.7 %collective-permute-start.37 = (bf16[256,640]{0,1:T(8,128)(2,1)S(1)}, bf16[256,640]{0,1:T(8,128)(2,1)S(1)}, u32[]{:S(2)}, u32[]{:S(2)}) collective-permute-start(bf16[256,640]{0,1:T(8,128)(2,1)S(1)} %get-tuple-element.44), channel_id=1, source_target_pairs={{0,6},{2,0},{4,2},{6,4},{1,7},{3,1},{5,3},{7,5},{8,14},{10,8},{12,... | collective-permute-start | bytes 983048 | tf_op jit(solution)/shard_map/ppermute | solution.py:44
  815.5 7.5 collective-permute-start.38
  816.9 9.5 %collective-permute-start.39 = (bf16[256,640]{0,1:T(8,128)(2,1)S(1)}, bf16[256,640]{0,1:T(8,128)(2,1)S(1)}, u32[]{:S(2)}, u32[]{:S(2)}) collective-permute-start(bf16[256,640]{0,1:T(8,128)(2,1)S(1)} %get-tuple-element.44), channel_id=1, source_target_pairs={{0,2},{2,4},{4,6},{6,0},{1,3},{3,5},{5,7},{7,1},{8,10},{10,12},{12... | collective-permute-start | bytes 983048 | tf_op jit(solution)/shard_map/ppermute | solution.py:44
  828.9 19.9 %collective-permute-start.40 = (bf16[2,256,640]{1,2,0:T(8,128)(2,1)}, bf16[2,256,640]{1,2,0:T(8,128)(2,1)}, u32[]{:S(2)}, u32[]{:S(2)}) collective-permute-start(bf16[2,256,640]{1,2,0:T(8,128)(2,1)} %constant_dynamic-slice_fusion.1), channel_id=1, source_target_pairs={{0,1},{1,0},{2,3},{3,2},{4,5},{5,4},{6,7},{7,6},{8,9},{9,8},{10,11... | collective-permute-start | bytes 1966088 | tf_op jit(solution)/shard_map/ppermute | solution.py:40
  (93 other events, 1567.3 us)
Sparse Core Ops, SparseCore 0:
  21.6 46.7 all-gather.7
  70.6 56.2 all-gather.13
  128.4 51.4 all-gather.11
  181.4 51.4 all-gather.9
  417.3 41.7 reduce-scatter.6
  462.7 202.1 all-gather.15
  667.9 41.1 reduce-scatter.8
  712.1 44.5 reduce-scatter.10
  759.2 43.4 reduce-scatter.4
